TPU v7x, 256 devices: a whole 4x4x8 slice. The times are simulated.
256 devices in a mesh: lon: 16 (over x, y_lo, core), lat: 16 (over y_hi, z).
Axes of the slice: x: 4, y: 4 (y_hi: 2, y_lo: 2; y = y_hi * 2 + y_lo), z: 8, core: 2. Of those that a mesh axis runs over, the one named last changes fastest.
Arguments:
- fields_in: bfloat16 [64, 512, 2048], P(None, 'lat', 'lon'), may hold values from -6 to 6
- weight_one: bfloat16 [3, 3, 64, 64], replicated, may hold values from -0.25 to 0.25
- weight_two: bfloat16 [3, 3, 64, 64], replicated, may hold values from -0.25 to 0.25
- cotangent: bfloat16 [64, 512, 2048], P(None, 'lat', 'lon'), may hold values from -6 to 6
- north_map: int32 [16], replicated, may hold values from 0 to 15, each once
- north_code: int32 [16], replicated, may hold values from 0 to 1
- south_map: int32 [16], replicated, may hold values from 0 to 15, each once
- south_code: int32 [16], replicated, may hold values from 0 to 1
Outputs:
- output: bfloat16 [64, 512, 2048], P(None, 'lat', 'lon')
- d_fields: bfloat16 [64, 512, 2048], P(None, 'lat', 'lon')
- grad_one: float32 [3, 3, 64, 64], replicated
- grad_two: float32 [3, 3, 64, 64], replicated
Inputs may be any that keep to these rules, and one draw needn't show every extreme that they name: north_map holds each longitude tile index once. south_map holds each longitude tile index once.
All inputs are finite; a program needn't handle non-finite values.
Results may differ from a plain program's by a relative error of at most 0.005.
Values may be sent and summed in bfloat16 or wider, within the bound.
A program may use at most 64 MiB of HBM per device.

v0:
```python
import jax
import jax.numpy as jnp
from jax import lax
from jax.sharding import PartitionSpec as P


def extended(block, sides, width, periodic):
    for axis, dim in sides:
        count = lax.axis_size(axis)
        forward = [(i, i + 1) for i in range(count - 1)]
        if periodic:
            forward.append((count - 1, 0))
        backward = [(target, source) for source, target in forward]
        low = lax.ppermute(
            lax.slice_in_dim(block, block.shape[dim] - width, None, axis=dim), axis, forward
        )
        high = lax.ppermute(lax.slice_in_dim(block, 0, width, axis=dim), axis, backward)
        block = jnp.concatenate([low, block, high], axis=dim)
    return block


def shifted(x, axis, by):
    size = lax.axis_size(axis)
    return lax.ppermute(x, axis, [(i, (i + by) % size) for i in range(size)])


def shifted_2(x, axis, by):
    size = lax.axis_size(axis)
    pairs = [(i, i + by) for i in range(size) if 0 <= i + by < size]
    return lax.ppermute(x, axis, pairs)


def pole_context(north_map, north_code, south_map, south_code):
    lat_count = lax.axis_size("lat")
    lat_place = lax.axis_index("lat")
    at_top = lat_place == 0
    at_bottom = lat_place == lat_count - 1
    partner = jnp.where(at_top, north_map, south_map)
    code_row = jnp.where(at_top, north_code, south_code)
    return (at_top, at_bottom, partner, code_row)


def extend(values, context):
    at_top, at_bottom, partner, code_row = context
    lon_count = lax.axis_size("lon")
    lon_place = lax.axis_index("lon")
    edge_row = jnp.where(at_top, values[:, 0, :], values[:, -1, :])
    gathered = lax.all_gather(edge_row[None], "lon", axis=0, tiled=True)
    chooser = (partner[:, None] == jnp.arange(lon_count, dtype=jnp.int32)[None, :]).astype(
        values.dtype
    )
    strips = jnp.einsum(
        "bj,jcq->bcq", chooser, gathered, preferred_element_type=jnp.float32
    ).astype(values.dtype)
    strips = jnp.where((code_row == 1)[:, None, None], strips[:, :, ::-1], strips)
    own_strip = lax.dynamic_index_in_dim(strips, lon_place, 0, keepdims=False)
    west_strip = lax.dynamic_index_in_dim(
        strips, (lon_place + lon_count - 1) % lon_count, 0, keepdims=False
    )
    east_strip = lax.dynamic_index_in_dim(strips, (lon_place + 1) % lon_count, 0, keepdims=False)
    polar_line = jnp.concatenate([west_strip[:, -1:], own_strip, east_strip[:, :1]], axis=1)
    widened = extended(values, (("lon", 2),), 1, True)
    padded = extended(widened, (("lat", 1),), 1, False)
    padded = padded.at[:, 0, :].set(jnp.where(at_top, polar_line, padded[:, 0, :]))
    padded = padded.at[:, -1, :].set(jnp.where(at_bottom, polar_line, padded[:, -1, :]))
    return padded


def fold_back(d_pad, context):
    at_top, at_bottom, partner, code_row = context
    lon_place = lax.axis_index("lon")
    from_east = shifted(d_pad[:, :, 0], "lon", -1)
    from_west = shifted(d_pad[:, :, -1], "lon", 1)
    inner_part = d_pad[:, :, 1:-1]
    inner_part = inner_part.at[:, :, -1].add(from_east)
    inner_part = inner_part.at[:, :, 0].add(from_west)
    from_below = shifted_2(inner_part[:, 0, :], "lat", -1)
    from_above = shifted_2(inner_part[:, -1, :], "lat", 1)
    rim_row = jnp.where(at_top, inner_part[:, 0, :], inner_part[:, -1, :])
    core_field = inner_part[:, 1:-1, :]
    core_field = core_field.at[:, -1, :].add(from_below)
    core_field = core_field.at[:, 0, :].add(from_above)
    rim_rows = lax.all_gather(rim_row[None], "lon", axis=0, tiled=True)
    rim_rows = jnp.where((code_row == 1)[:, None, None], rim_rows[:, :, ::-1], rim_rows)
    matches = (partner == lon_place)[:, None, None]
    arriving = jnp.sum(jnp.where(matches, rim_rows, 0.0), axis=0)
    core_field = core_field.at[:, 0, :].add(jnp.where(at_top, arriving, 0.0))
    core_field = core_field.at[:, -1, :].add(jnp.where(at_bottom, arriving, 0.0))
    return core_field


def convolve(padded, weight):
    result = lax.conv_general_dilated(
        padded[None],
        weight,
        (1, 1),
        "VALID",
        dimension_numbers=("NCHW", "HWOI", "NCHW"),
        preferred_element_type=jnp.float32,
    )
    return result[0]


def back_conv(upstream, weight, padded, row_count, col_count):
    flipped = weight[::-1, ::-1]
    d_pad = lax.conv_general_dilated(
        upstream[None],
        flipped,
        (1, 1),
        ((2, 2), (2, 2)),
        dimension_numbers=("NCHW", "HWIO", "NCHW"),
        preferred_element_type=jnp.float32,
    )[0]
    grads = []
    for shift_row in range(3):
        for shift_col in range(3):
            window = padded[:, shift_row : shift_row + row_count, shift_col : shift_col + col_count]
            grads.append(
                jnp.einsum("orq,crq->oc", upstream, window, preferred_element_type=jnp.float32)
            )
    return (d_pad, jnp.stack(grads).reshape(3, 3, weight.shape[2], weight.shape[3]))


def on_device(
    fields_in, weight_one, weight_two, cotangent, north_map, north_code, south_map, south_code
):
    row_count = fields_in.shape[1]
    col_count = fields_in.shape[2]
    pixel_total = row_count * col_count * lax.axis_size("lon") * lax.axis_size("lat")
    grad_scale = 1.0 / jnp.sqrt(jnp.float32(pixel_total))
    context = pole_context(north_map, north_code, south_map, south_code)
    padded_in = extend(fields_in, context)
    pre_act = convolve(padded_in, weight_one)
    hidden = jax.nn.gelu(pre_act).astype(jnp.bfloat16)
    padded_hidden = extend(hidden, context)
    output = convolve(padded_hidden, weight_two).astype(jnp.bfloat16)
    spread_two, local_two = back_conv(cotangent, weight_two, padded_hidden, row_count, col_count)
    back_hidden = fold_back(spread_two, context)
    _, pull_gelu = jax.vjp(jax.nn.gelu, pre_act)
    d_pre = pull_gelu(back_hidden)[0].astype(jnp.bfloat16)
    spread_one, local_one = back_conv(d_pre, weight_one, padded_in, row_count, col_count)
    d_fields = fold_back(spread_one, context).astype(jnp.bfloat16)
    summed_one, summed_two = lax.psum((local_one, local_two), ("lon", "lat"))
    grad_one = summed_one * grad_scale
    grad_two = summed_two * grad_scale
    return (output, d_fields, grad_one, grad_two)


def solution(mesh):
    placed = (P(None, "lat", "lon"), P(), P(), P(None, "lat", "lon"), P(), P(), P(), P())
    return jax.shard_map(
        on_device,
        mesh=mesh,
        in_specs=placed,
        out_specs=(P(None, "lat", "lon"), P(None, "lat", "lon"), P(), P()),
        check_vma=False,
    )
```

profile of v0, /device:TPU:1, one launch (start us, length us, event | category | flops | bytes accessed | tf_op | source)
XLA Modules:
  0.0 512.9 jit_solution(16503765228283339314)
XLA Ops:
  9.7 2.7 collective-permute-start
  12.9 1.7 copy.156
  15.8 1.8 convolution_select_fusion.1
  18.1 1.7 slice.577
  19.8 3.7 copy.193
  25.8 2.8 collective-permute-start.8
  28.5 20.2 %all-gather = bf16[1024,1,128]{2,0,1:T(8,128)(2,1)S(1)} all-gather(bf16[64,1,128]{2,0,1:T(8,128)(2,1)S(1)} %slice_select_fusion.5), channel_id=2, replica_groups=mesh['lon'=16,'lat'=16] {'lon'}, dimensions={0}, use_global_device_ids=true | all-gather | bytes 278528 | tf_op jit(solution)/shard_map/all_gather | solution.py:48
  49.7 1.4 slice.578
  51.1 1.5 pad_maximum_fusion.7
  52.6 1.8 collective-permute-start.2
  54.4 1.8 collective-permute-start.3
  56.2 2.2 copy.161
  58.3 2.4 slice_add_fusion.3
  62.0 8.3 %scatter-add.40 = f32[64,34,128]{2,0,1:T(8,128)S(1)} dynamic-update-slice(f32[64,34,128]{2,0,1:T(8,128)S(1)} %copy-done.3, f32[64,34,1]{2,0,1:T(8,128)} %slice_add_fusion.3, s32[]{:T(128)} %constant.407.clone.1, s32[]{:T(128)} %constant.407.clone.1, s32[]{:T(128)} %constant.417.clone.1) | dynamic-update-slice | bytes 17412 | tf_op jit(solution)/shard_map/scatter-add | solution.py:75
  71.6 5.8 %scatter-add.41 = f32[64,34,128]{2,0,1:T(8,128)S(1)} dynamic-update-slice(f32[64,34,128]{2,0,1:T(8,128)S(1)} %scatter-add.40, f32[64,34,1]{2,0,1:T(8,128)} %slice_add_fusion.2, s32[]{:T(128)} %constant.407.clone.1, s32[]{:T(128)} %constant.407.clone.1, s32[]{:T(128)} %constant.407.clone.1) | dynamic-update-slice | bytes 17412 | tf_op jit(solution)/shard_map/scatter-add | solution.py:76
  78.0 4.2 collective-permute-start.11
  82.1 1.3 collective-permute-start.10
  83.4 20.3 %all-gather.2 = f32[1024,1,128]{2,0,1:T(8,128)S(1)} all-gather(f32[64,1,128]{2,0,1:T(8,128)S(1)} %get-tuple-element.227), channel_id=4, replica_groups=mesh['lon'=16,'lat'=16] {'lon'}, dimensions={0}, use_global_device_ids=true | all-gather | bytes 557056 | tf_op jit(solution)/shard_map/all_gather | solution.py:83
  105.7 1.8 pad_maximum_fusion
  108.7 3.0 copy.195
  112.7 2.8 convolution_select_fusion.2
  116.0 1.5 slice.566
  117.5 3.8 copy.192
  125.3 17.1 %all-gather.1 = bf16[1024,1,128]{2,0,1:T(8,128)(2,1)S(1)} all-gather(bf16[64,1,128]{2,0,1:T(8,128)(2,1)S(1)} %slice_select_fusion.4), channel_id=3, replica_groups=mesh['lon'=16,'lat'=16] {'lon'}, dimensions={0}, use_global_device_ids=true | all-gather | bytes 278528 | tf_op jit(solution)/shard_map/all_gather | solution.py:48
  147.4 1.6 copy.196
  149.8 1.6 collective-permute-start.4
  151.4 1.8 convolution_select_fusion
  153.8 1.7 slice.590
  155.4 3.7 copy.194
  160.1 1.4 slice.591
  161.5 1.7 collective-permute-start.13
  164.2 1.7 collective-permute-done.5
  165.9 1.5 pad_maximum_fusion.4
  167.4 4.0 collective-permute-start.6
  172.8 1.4 copy.170
  174.2 2.4 slice_add_fusion.1
  177.9 8.3 %scatter-add.50 = f32[64,34,128]{2,0,1:T(8,128)S(1)} dynamic-update-slice(f32[64,34,128]{2,0,1:T(8,128)S(1)} %copy-done.2, f32[64,34,1]{2,0,1:T(8,128)} %slice_add_fusion.1, s32[]{:T(128)} %constant.407.clone.1, s32[]{:T(128)} %constant.407.clone.1, s32[]{:T(128)} %constant.417.clone.1) | dynamic-update-slice | bytes 17412 | tf_op jit(solution)/shard_map/scatter-add | solution.py:75
  187.4 5.8 %scatter-add.51 = f32[64,34,128]{2,0,1:T(8,128)S(1)} dynamic-update-slice(f32[64,34,128]{2,0,1:T(8,128)S(1)} %scatter-add.50, f32[64,34,1]{2,0,1:T(8,128)} %slice_add_fusion, s32[]{:T(128)} %constant.407.clone.1, s32[]{:T(128)} %constant.407.clone.1, s32[]{:T(128)} %constant.407.clone.1) | dynamic-update-slice | bytes 17412 | tf_op jit(solution)/shard_map/scatter-add | solution.py:76
  193.2 5.3 %collective-permute-start.15 = (f32[64,128]{1,0:T(8,128)S(1)}, f32[64,128]{1,0:T(8,128)S(1)}, u32[]{:S(2)}, u32[]{:S(2)}) collective-permute-start(f32[64,128]{1,0:T(8,128)S(1)} %get-tuple-element.225), channel_id=1, source_target_pairs={{0,1},{1,2},{2,3},{3,4},{4,5},{5,6},{6,7},{7,8},{8,9},{9,10},{10,1... | collective-permute-start | bytes 98312 | tf_op jit(solution)/shard_map/ppermute | solution.py:30
  199.8 20.0 %all-gather.3 = f32[1024,1,128]{2,0,1:T(8,128)S(1)} all-gather(f32[64,1,128]{2,0,1:T(8,128)S(1)} %get-tuple-element.224), channel_id=5, replica_groups=mesh['lon'=16,'lat'=16] {'lon'}, dimensions={0}, use_global_device_ids=true | all-gather | bytes 557056 | tf_op jit(solution)/shard_map/all_gather | solution.py:83
  223.7 1.7 pad_maximum_fusion.1
  228.8 3.0 copy.197
  233.0 2.8 select_convert_fusion
  237.2 1.6 fusion.28
  239.7 3.7 copy.184
  244.8 257.5 %all-reduce.3.cloned.1.call-done = (f32[3,3,64,64]{3,2,1,0:T(8,128)}, f32[3,3,64,64]{3,2,1,0:T(8,128)}) async-done(((f32[3,3,64,64]{3,2,1,0:T(8,128)}, f32[3,3,64,64]{3,2,1,0:T(8,128)}), (f32[3,3,64,64]{3,2,1,0:T(8,128)}, f32[3,3,64,64]{3,2,1,0:T(8,128)})) %all-reduce.3.cloned.1.call-update) | async-done | bytes 294928 | tf_op jit(solution)/shard_map/psum | solution.py:143
  502.3 1.7 broadcast_multiply_fusion.1
  504.0 1.7 broadcast_multiply_fusion
  (175 shorter events, 44.2 us)
Async XLA Ops:
  7.2 105.0 %copy-start = (bf16[3,3,64,64]{3,2,1,0:T(8,128)(2,1)S(1)}, bf16[3,3,64,64]{3,2,1,0:T(8,128)(2,1)}, u32[]{:S(2)}) copy-start(bf16[3,3,64,64]{3,2,1,0:T(8,128)(2,1)} %param.41) | copy-start | bytes 221188
  7.2 495.1 %all-reduce.3.cloned.1.call-start = ((), (), s32[]{:S(2)}) async-start(), calls=%async_computation | async-start | bytes 1179648 | tf_op jit(solution)/shard_map/psum | solution.py:143
  8.5 4.4 copy-start.10
  9.7 41.4 %collective-permute-start = (bf16[64,32,1]{2,0,1:T(8,128)(2,1)}, bf16[64,32,1]{2,0,1:T(8,128)(2,1)}, u32[]{:S(2)}, u32[]{:S(2)}) collective-permute-start(bf16[64,32,1]{2,0,1:T(8,128)(2,1)} %get-tuple-element.234), channel_id=1, source_target_pairs={{0,16},{16,32},{32,48},{48,64},{64,80},{80,96},{96,112},{112,128},... | collective-permute-start | bytes 12296 | tf_op jit(solution)/shard_map/ppermute | solution.py:14
  12.4 38.7 %collective-permute-start.1 = (bf16[64,32,1]{2,0,1:T(8,128)(2,1)}, bf16[64,32,1]{2,0,1:T(8,128)(2,1)}, u32[]{:S(2)}, u32[]{:S(2)}) collective-permute-start(bf16[64,32,1]{2,0,1:T(8,128)(2,1)} %get-tuple-element.235), channel_id=1, source_target_pairs={{16,0},{32,16},{48,32},{64,48},{80,64},{96,80},{112,96},{128,112},... | collective-permute-start | bytes 12296 | tf_op jit(solution)/shard_map/ppermute | solution.py:17
  14.9 0.9 copy-start.24
  14.9 0.9 copy-start.28
  23.5 25.3 %copy-start.20 = (s32[16]{0:T(128)S(1)}, s32[16]{0:T(128)}, u32[]{:S(2)}) copy-start(s32[16]{0:T(128)} %param.44) | copy-start | bytes 196
  23.5 25.3 %copy-start.21 = (s32[16]{0:T(128)S(1)}, s32[16]{0:T(128)}, u32[]{:S(2)}) copy-start(s32[16]{0:T(128)} %param.46) | copy-start | bytes 196
  23.5 25.3 %copy-start.22 = (s32[16]{0:T(128)S(1)}, s32[16]{0:T(128)}, u32[]{:S(2)}) copy-start(s32[16]{0:T(128)} %param.45) | copy-start | bytes 196
  23.5 25.3 %copy-start.23 = (s32[16]{0:T(128)S(1)}, s32[16]{0:T(128)}, u32[]{:S(2)}) copy-start(s32[16]{0:T(128)} %param.47) | copy-start | bytes 196
  24.5 36.3 %collective-permute-start.9 = (f32[64,34]{0,1:T(8,128)S(1)}, f32[64,34]{0,1:T(8,128)S(1)}, u32[]{:S(2)}, u32[]{:S(2)}) collective-permute-start(f32[64,34]{0,1:T(8,128)S(1)} %get-tuple-element.214), channel_id=1, source_target_pairs={{0,16},{16,32},{32,48},{48,64},{64,80},{80,96},{96,112},{112,128},... | collective-permute-start | bytes 26120 | tf_op jit(solution)/shard_map/ppermute | solution.py:24
  25.8 30.4 %collective-permute-start.8 = (f32[64,34]{0,1:T(8,128)S(1)}, f32[64,34]{0,1:T(8,128)}, u32[]{:S(2)}, u32[]{:S(2)}) collective-permute-start(f32[64,34]{0,1:T(8,128)S(1)} %get-tuple-element.215), channel_id=1, source_target_pairs={{0,240},{16,0},{32,16},{48,32},{64,48},{80,64},{96,80},{112,96},{1... | collective-permute-start | bytes 26120 | tf_op jit(solution)/shard_map/ppermute | solution.py:24
  48.8 2.2 copy-start.18
  48.8 55.4 %copy-start.16 = (pred[16]{0:T(512)(128)(4,1)}, pred[16]{0:T(512)(128)(4,1)S(1)}, u32[]{:S(2)}) copy-start(pred[16]{0:T(512)(128)(4,1)S(1)} %get-tuple-element.218) | copy-start | bytes 52
  48.8 94.0 %copy-start.14 = (pred[16]{0:T(512)(128)(4,1)}, pred[16]{0:T(512)(128)(4,1)S(1)}, u32[]{:S(2)}) copy-start(pred[16]{0:T(512)(128)(4,1)S(1)} %get-tuple-element.242) | copy-start | bytes 52
  52.6 53.1 %collective-permute-start.2 = (bf16[64,1,130]{2,0,1:T(8,128)(2,1)}, bf16[64,1,130]{2,0,1:T(8,128)(2,1)S(1)}, u32[]{:S(2)}, u32[]{:S(2)}) collective-permute-start(bf16[64,1,130]{2,0,1:T(8,128)(2,1)} %get-tuple-element.222), channel_id=1, source_target_pairs={{0,1},{1,2},{2,3},{3,4},{4,5},{5,6},{6,7},{7,8},{8,9},{9,10},{10,1... | collective-permute-start | bytes 49928 | tf_op jit(solution)/shard_map/ppermute | solution.py:14
  54.4 51.3 %collective-permute-start.3 = (bf16[64,1,130]{2,0,1:T(8,128)(2,1)}, bf16[64,1,130]{2,0,1:T(8,128)(2,1)S(1)}, u32[]{:S(2)}, u32[]{:S(2)}) collective-permute-start(bf16[64,1,130]{2,0,1:T(8,128)(2,1)} %get-tuple-element.223), channel_id=1, source_target_pairs={{1,0},{2,1},{3,2},{4,3},{5,4},{6,5},{7,6},{8,7},{9,8},{10,9},{11,1... | collective-permute-start | bytes 49928 | tf_op jit(solution)/shard_map/ppermute | solution.py:17
  60.8 1.2 copy-start.3
  78.0 44.2 %collective-permute-start.11 = (f32[64,128]{1,0:T(8,128)S(1)}, f32[64,128]{1,0:T(8,128)S(1)}, u32[]{:S(2)}, u32[]{:S(2)}) collective-permute-start(f32[64,128]{1,0:T(8,128)S(1)} %get-tuple-element.228), channel_id=1, source_target_pairs={{0,1},{1,2},{2,3},{3,4},{4,5},{5,6},{6,7},{7,8},{8,9},{9,10},{10,1... | collective-permute-start | bytes 98312 | tf_op jit(solution)/shard_map/ppermute | solution.py:30
  82.1 39.1 %collective-permute-start.10 = (f32[64,128]{1,0:T(8,128)}, f32[64,128]{1,0:T(8,128)}, u32[]{:S(2)}, u32[]{:S(2)}) collective-permute-start(f32[64,128]{1,0:T(8,128)} %get-tuple-element.229), channel_id=1, source_target_pairs={{1,0},{2,1},{3,2},{4,3},{5,4},{6,5},{7,6},{8,7},{9,8},{10,9},{11,1... | collective-permute-start | bytes 98312 | tf_op jit(solution)/shard_map/ppermute | solution.py:30
  107.7 1.0 copy-start.4
  112.0 0.7 copy-start.26
  117.5 3.8 copy-start.8
  122.0 1.2 copy-start.9
  124.1 18.3 %copy-start.19 = (s32[16]{0:T(128)S(1)}, s32[16]{0:T(128)}, u32[]{:S(2)}) copy-start(s32[16]{0:T(128)} %copy-done.18) | copy-start | bytes 196
  142.4 1.2 copy-start.5
  146.7 0.7 copy-start.13
  149.3 2.1 copy-start.29
  149.8 14.5 %collective-permute-start.4 = (bf16[64,32,1]{2,0,1:T(8,128)(2,1)}, bf16[64,32,1]{2,0,1:T(8,128)(2,1)S(1)}, u32[]{:S(2)}, u32[]{:S(2)}) collective-permute-start(bf16[64,32,1]{2,0,1:T(8,128)(2,1)} %get-tuple-element.232), channel_id=1, source_target_pairs={{0,16},{16,32},{32,48},{48,64},{64,80},{80,96},{96,112},{112,128},... | collective-permute-start | bytes 12296 | tf_op jit(solution)/shard_map/ppermute | solution.py:14
  151.4 14.5 %collective-permute-start.5 = (bf16[64,32,1]{2,0,1:T(8,128)(2,1)}, bf16[64,32,1]{2,0,1:T(8,128)(2,1)}, u32[]{:S(2)}, u32[]{:S(2)}) collective-permute-start(bf16[64,32,1]{2,0,1:T(8,128)(2,1)} %get-tuple-element.233), channel_id=1, source_target_pairs={{16,0},{32,16},{48,32},{64,48},{80,64},{96,80},{112,96},{128,112},... | collective-permute-start | bytes 12296 | tf_op jit(solution)/shard_map/ppermute | solution.py:17
  161.5 15.2 %collective-permute-start.13 = (f32[64,34]{0,1:T(8,128)S(1)}, f32[64,34]{0,1:T(8,128)S(1)}, u32[]{:S(2)}, u32[]{:S(2)}) collective-permute-start(f32[64,34]{0,1:T(8,128)S(1)} %get-tuple-element.212), channel_id=1, source_target_pairs={{0,16},{16,32},{32,48},{48,64},{64,80},{80,96},{96,112},{112,128},... | collective-permute-start | bytes 26120 | tf_op jit(solution)/shard_map/ppermute | solution.py:24
  163.2 9.5 %collective-permute-start.12 = (f32[64,34]{0,1:T(8,128)S(1)}, f32[64,34]{0,1:T(8,128)S(1)}, u32[]{:S(2)}, u32[]{:S(2)}) collective-permute-start(f32[64,34]{0,1:T(8,128)S(1)} %get-tuple-element.213), channel_id=1, source_target_pairs={{0,240},{16,0},{32,16},{48,32},{64,48},{80,64},{96,80},{112,96},{1... | collective-permute-start | bytes 26120 | tf_op jit(solution)/shard_map/ppermute | solution.py:24
  167.4 56.2 %collective-permute-start.6 = (bf16[64,1,130]{2,0,1:T(8,128)(2,1)}, bf16[64,1,130]{2,0,1:T(8,128)(2,1)S(1)}, u32[]{:S(2)}, u32[]{:S(2)}) collective-permute-start(bf16[64,1,130]{2,0,1:T(8,128)(2,1)} %get-tuple-element.220), channel_id=1, source_target_pairs={{0,1},{1,2},{2,3},{3,4},{4,5},{5,6},{6,7},{7,8},{8,9},{9,10},{10,1... | collective-permute-start | bytes 49928 | tf_op jit(solution)/shard_map/ppermute | solution.py:14
  171.5 52.2 %collective-permute-start.7 = (bf16[64,1,130]{2,0,1:T(8,128)(2,1)}, bf16[64,1,130]{2,0,1:T(8,128)(2,1)S(1)}, u32[]{:S(2)}, u32[]{:S(2)}) collective-permute-start(bf16[64,1,130]{2,0,1:T(8,128)(2,1)} %get-tuple-element.221), channel_id=1, source_target_pairs={{1,0},{2,1},{3,2},{4,3},{5,4},{6,5},{7,6},{8,7},{9,8},{10,9},{11,1... | collective-permute-start | bytes 49928 | tf_op jit(solution)/shard_map/ppermute | solution.py:17
  176.7 1.2 copy-start.2
  193.2 50.3 %collective-permute-start.15 = (f32[64,128]{1,0:T(8,128)S(1)}, f32[64,128]{1,0:T(8,128)S(1)}, u32[]{:S(2)}, u32[]{:S(2)}) collective-permute-start(f32[64,128]{1,0:T(8,128)S(1)} %get-tuple-element.225), channel_id=1, source_target_pairs={{0,1},{1,2},{2,3},{3,4},{4,5},{5,6},{6,7},{7,8},{8,9},{9,10},{10,1... | collective-permute-start | bytes 98312 | tf_op jit(solution)/shard_map/ppermute | solution.py:30
  198.5 44.9 %collective-permute-start.14 = (f32[64,128]{1,0:T(8,128)S(1)}, f32[64,128]{1,0:T(8,128)S(1)}, u32[]{:S(2)}, u32[]{:S(2)}) collective-permute-start(f32[64,128]{1,0:T(8,128)S(1)} %get-tuple-element.226), channel_id=1, source_target_pairs={{1,0},{2,1},{3,2},{4,3},{5,4},{6,5},{7,6},{8,7},{9,8},{10,9},{11,1... | collective-permute-start | bytes 98312 | tf_op jit(solution)/shard_map/ppermute | solution.py:30
  219.8 2.3 copy-start.15
  219.8 2.4 copy-start.17
  223.6 1.9 copy-start.11
  225.6 2.8 copy-start.6
  232.1 0.9 copy-start.25
  232.1 0.9 copy-start.27
  236.0 1.2 copy-start.12
  239.7 3.7 copy-start.7
  243.6 262.1 %copy-start.1 = (bf16[3,3,64,64]{3,2,1,0:T(8,128)(2,1)S(1)}, bf16[3,3,64,64]{3,2,1,0:T(8,128)(2,1)}, u32[]{:S(2)}) copy-start(bf16[3,3,64,64]{3,2,1,0:T(8,128)(2,1)} %param.41) | copy-start | bytes 221188
Sparse Core Ops, SparseCore 0:
  243.5 258.7 all-reduce.2
where the time goes:
time: 523 us; the launch traced here: 513 us
  waiting for transfers between devices  259 us (50%)
  local copies, waits for them, and re-layouts  89.5 us (17%)
  blocking collectives  77.7 us (15%)
  starting transfers between devices  32.6 us (6%)
  other arithmetic  20.8 us (4%)
  matrix products  17.7 us (3%)
  between operations  15.4 us (3%)
    psum x1, waiting for transfers between devices, on_device(): summed_one, summed_two = lax.psum((local_one, local_two), ('lon', 'lat'))  258 us
    all_gather x2, blocking collectives, fold_back(): rim_rows = lax.all_gather(rim_row[None], 'lon', axis=0, tiled=True)  40.3 us
    all_gather x2, blocking collectives, extend(): gathered = lax.all_gather(edge_row[None], 'lon', axis=0, tiled=True)  37.4 us
    unnamed x78, local copies, waits for them, and re-layouts  33.5 us
    scatter-add x2, local copies, waits for them, and re-layouts, fold_back(): inner_part = inner_part.at[:, :, -1].add(from_east)  16.7 us
    ppermute x4, starting transfers between devices, shifted_2(): return lax.ppermute(x, axis, pairs)  12 us
    scatter-add x2, local copies, waits for them, and re-layouts, fold_back(): inner_part = inner_part.at[:, :, 0].add(from_west)  11.5 us
  transfers between devices with their start and end apart: 17, of which 2 were waited for; matrix products, arithmetic and copies ran while one was open for 21% of the time, Pallas kernels for 0%

commit v1 on v0

v1 whole, which is shorter than its diff:
```python
import functools
import math

import jax
import jax.numpy as jnp
from jax import lax
from jax.experimental import pallas as pl
from jax.experimental.pallas import tpu as pltpu
from jax.sharding import PartitionSpec as P

MESH = pl.DeviceIdType.MESH
LANES = 128
F32 = jnp.float32
BF16 = jnp.bfloat16


def lane_index(shape):
    return lax.broadcasted_iota(jnp.int32, shape, len(shape) - 1)


def aligned(start, step):
    return pl.multiple_of(start * step, step)


def kernel(
    nlon, nlat, rows, chans, owners, scale,
    fields_ref, cot_ref, w_ref, north_map, north_code, south_map, south_code,
    out_ref, df_ref, g1_ref, g2_ref,
    stage, fwide, gwide, hwide, dwide, slope, wedge,
    send_a, recv_a, pole_a, send_b, recv_b, pole_b, send_c, recv_c, pole_c,
    acc_one, acc_two, rs_send, rs_recv, ar_send, ar_recv, ag_buf,
    near_send, near_recv, pole_send, pole_recv,
    rs_ssem, rs_rsem, ar_ssem, ar_rsem, ag_ssem, ag_rsem,
):
    lon = lax.axis_index("lon")
    lat = lax.axis_index("lat")
    west = lax.rem(lon + nlon - 1, nlon)
    east = lax.rem(lon + 1, nlon)
    has_north = lat > 0
    has_south = lat < nlat - 1
    at_top = lat == 0
    at_pole = jnp.logical_or(lat == 0, lat == nlat - 1)
    at_bottom = lat == nlat - 1
    lane = lane_index((chans, LANES))
    own_rows = pl.ds(0, LANES)
    ghost_cols = pl.ds(LANES, LANES)
    piece = ag_buf.shape[0] // owners

    def other(k, me, count):
        return lax.rem(me + k, count)

    barrier = pltpu.get_barrier_semaphore()

    def greet(lat_at, lon_at):
        pl.semaphore_signal(
            barrier, inc=1, device_id={"lon": lon_at, "lat": lat_at}, device_id_type=MESH
        )

    def greet_lon(k, c):
        greet(lat, other(k, lon, nlon))
        return c

    def greet_lat(k, c):
        greet(other(k, lat, nlat), lon)
        return c

    lax.fori_loop(1, nlon, greet_lon, 0)
    lax.fori_loop(1, nlat, greet_lat, 0)

    @pl.when(has_north)
    def _():
        greet(lat - 1, west)
        greet(lat - 1, east)

    @pl.when(has_south)
    def _():
        greet(lat + 1, west)
        greet(lat + 1, east)

    diagonals = 2 * has_north.astype(jnp.int32) + 2 * has_south.astype(jnp.int32)

    def put(src, dst, ssem, rsem, lat_at, lon_at):
        return pltpu.make_async_remote_copy(
            src_ref=src, dst_ref=dst, send_sem=ssem, recv_sem=rsem,
            device_id={"lon": lon_at, "lat": lat_at}, device_id_type=MESH,
        )

    def near_copies(x, send, recv):
        def one(part, slot, at, lat_at, lon_at):
            return put(
                send.at[part], recv.at[slot], near_send.at[x, at], near_recv.at[x, slot],
                lat_at, lon_at,
            )

        sides = [one(2, 1, 0, lat, west), one(2, 0, 1, lat, east)]
        up = [
            one(0, 7, 2, lat - 1, west), one(0, 6, 3, lat - 1, lon), one(0, 5, 4, lat - 1, east)
        ]
        down = [
            one(1, 4, 5, lat + 1, west), one(1, 3, 6, lat + 1, lon), one(1, 2, 7, lat + 1, east)
        ]
        return sides, up, down

    def pole_copy(x, part, send, pole, k):
        target = other(k, lon, nlon)
        return put(
            send.at[part], pole.at[lon], pole_send.at[x, k], pole_recv.at[x, lon], lat, target
        )

    def start_exchange(x, send, recv, pole):
        sides, up, down = near_copies(x, send, recv)

        def pole_start(part):
            pole[lon] = send[part]

            def step(k, c):
                pole_copy(x, part, send, pole, k).start()
                return c

            lax.fori_loop(1, nlon, step, 0)

        @pl.when(at_top)
        def _():
            pole_start(0)

        @pl.when(at_bottom)
        def _():
            pole_start(1)

        for copy in sides:
            copy.start()

        @pl.when(has_north)
        def _():
            for copy in up:
                copy.start()

        @pl.when(has_south)
        def _():
            for copy in down:
                copy.start()

    def finish_exchange(x, send, recv, pole):
        sides, up, down = near_copies(x, send, recv)

        def arrived(slot):
            put(
                send.at[0], recv.at[slot], near_send.at[x, 0], near_recv.at[x, slot], lat, lon
            ).wait_recv()

        for copy in sides:
            copy.wait_send()
        arrived(0)
        arrived(1)

        @pl.when(has_north)
        def _():
            for copy in up:
                copy.wait_send()
            for slot in (2, 3, 4):
                arrived(slot)

        @pl.when(has_south)
        def _():
            for copy in down:
                copy.wait_send()
            for slot in (5, 6, 7):
                arrived(slot)

        @pl.when(at_pole)
        def _():
            def step(k, c):
                pole_copy(x, 0, send, pole, k).wait_send()
                source = other(k, lon, nlon)
                put(
                    send.at[0], pole.at[source], pole_send.at[x, k], pole_recv.at[x, source],
                    lat, lon,
                ).wait_recv()
                return c

            lax.fori_loop(1, nlon, step, 0)

    def map_at(k):
        return jnp.where(at_top, north_map[k], south_map[k])

    def code_at(k):
        return jnp.where(at_top, north_code[k], south_code[k])

    def owner_of_copy():
        def step(k, c):
            hit = map_at(k) == lon
            return jnp.where(hit, k, c[0]), jnp.where(hit, code_at(k), c[1])

        return lax.fori_loop(0, nlon, step, (jnp.int32(0), jnp.int32(0)))

    def turned(row, code):
        i = lax.broadcasted_iota(jnp.int32, (LANES, LANES), 0)
        j = lax.broadcasted_iota(jnp.int32, (LANES, LANES), 1)
        match = (i + (2 * code - 1) * j) == (LANES - 1) * code
        turn = jnp.where(match, 1.0, 0.0).astype(BF16)
        return jnp.dot(row, turn, preferred_element_type=F32)

    def set_ghost_row(wide, row, left, mid, right):
        place = pl.ds(row * chans, chans)
        wide[place, own_rows] = mid.astype(BF16)
        wide[place, ghost_cols] = jnp.where(lane == 0, right.astype(F32), left.astype(F32)).astype(
            BF16
        )

    def set_ghost_cols(wide, from_west, from_east):
        merged = jnp.where(lane % 2 == 0, from_east.astype(F32), from_west.astype(F32))

        def step(h, c):
            place = pl.ds(aligned(h + 1, chans), chans)
            wide[place, ghost_cols] = pltpu.roll(merged, lax.rem(LANES - 2 * h, LANES), 1).astype(
                BF16
            )
            return c

        lax.fori_loop(0, rows, step, 0, unroll=4)

    def edges_into(send, part, wide, packed):
        top, bottom, side = (
            (send.at[i] if part is None else send.at[i, part]) for i in range(3)
        )
        top[...] = wide[pl.ds(chans, chans), own_rows]
        bottom[...] = wide[pl.ds(rows * chans, chans), own_rows]
        side[...] = packed.astype(BF16)

    def pack_edge(h, value, packed):
        keep = jnp.logical_or(lane == 2 * h, lane == lax.rem(2 * h + LANES - 1, LANES))
        return jnp.where(keep, pltpu.roll(value, 2 * h, 1), packed)

    def take_in(source, wide, send, part):
        stage[...] = source[...].astype(F32)

        def step(h, packed):
            value = stage[pl.ds(h, chans, stride=rows), :]
            wide[pl.ds(aligned(h + 1, chans), chans), own_rows] = value.astype(BF16)
            return pack_edge(h, value, packed)

        packed = lax.fori_loop(0, rows, step, jnp.zeros((chans, LANES), F32), unroll=4)
        edges_into(send, part, wide, packed)

    def ghosts_forward(wide, recv, pole, part):
        def got(slot):
            return recv[slot] if part is None else recv[slot, part]

        def strip(k):
            index = map_at(k)
            row = pole[index] if part is None else pole[index, part]
            return turned(row, code_at(k))

        set_ghost_cols(wide, got(0), got(1))

        @pl.when(has_north)
        def _():
            set_ghost_row(wide, 0, got(2), got(3), got(4))

        @pl.when(has_south)
        def _():
            set_ghost_row(wide, rows + 1, got(5), got(6), got(7))

        @pl.when(at_top)
        def _():
            set_ghost_row(wide, 0, strip(west), strip(lon), strip(east))

        @pl.when(at_bottom)
        def _():
            set_ghost_row(wide, rows + 1, strip(west), strip(lon), strip(east))

    def ghosts_backward(wide, recv, pole, part):
        def got(slot):
            return recv[slot] if part is None else recv[slot, part]

        def rim(row):
            source, code = owner_of_copy()

            def strip(shift):
                index = lax.rem(source + shift + nlon, nlon)
                return turned(pole[index] if part is None else pole[index, part], code)

            before, mid, after = strip(-1), strip(0), strip(1)
            flip = code == 1
            set_ghost_row(
                wide, row, jnp.where(flip, after, before), mid, jnp.where(flip, before, after)
            )

        set_ghost_cols(wide, got(0), got(1))

        @pl.when(has_north)
        def _():
            set_ghost_row(wide, 0, got(2), got(3), got(4))

        @pl.when(has_south)
        def _():
            set_ghost_row(wide, rows + 1, got(5), got(6), got(7))

        @pl.when(at_top)
        def _():
            rim(0)

        @pl.when(at_bottom)
        def _():
            rim(rows + 1)

    def rim_weights():
        for kernel_at in range(2):
            base = w_ref[2 + kernel_at]
            for place in range(3):
                wedge[kernel_at * 3 + place] = base

            def replace(place, into, out_of):
                _, code = owner_of_copy()
                full = base.astype(F32)
                shown = lax.broadcasted_iota(jnp.int32, full.shape, 1) // chans == into
                width = full.shape[1]
                i = lax.broadcasted_iota(jnp.int32, (width, width), 0)
                j = lax.broadcasted_iota(jnp.int32, (width, width), 1)
                move = jnp.where(i - out_of * chans == j - into * chans, 1.0, 0.0).astype(BF16)
                moved = jnp.dot(base, move, preferred_element_type=F32)
                swapped = jnp.concatenate(
                    [moved[2 * chans :], moved[chans : 2 * chans], moved[:chans]], axis=0
                )
                chosen = jnp.where(code == 1, swapped, moved)
                wedge[kernel_at * 3 + place] = jnp.where(shown, chosen, full).astype(BF16)

            @pl.when(at_top)
            def _():
                replace(0, 0, 2)

            @pl.when(at_bottom)
            def _():
                replace(2, 2, 0)

    def conv_row(weights, wide, h):
        window = wide[pl.ds(aligned(h, chans), 3 * chans), :]
        y = jnp.dot(weights, window, preferred_element_type=F32)
        left = jnp.where(lane == LANES - 1, y[:chans, LANES:], y[:chans, :LANES])
        right = jnp.where(lane == 0, y[2 * chans :, LANES:], y[2 * chans :, :LANES])
        return (
            pltpu.roll(left, 1, 1) + y[chans : 2 * chans, :LANES] + pltpu.roll(right, LANES - 1, 1)
        )

    def gradient(up_wide, wide, acc):
        group = 4

        def shifted(h):
            g = up_wide[pl.ds(aligned(h + 1, chans), chans), own_rows].astype(F32)
            ahead = pltpu.roll(g, LANES - 1, 1)
            behind = pltpu.roll(g, 1, 1)
            zero = jnp.zeros_like(g)
            first = jnp.concatenate(
                [jnp.where(lane != LANES - 1, ahead, zero), g, jnp.where(lane != 0, behind, zero)],
                axis=0,
            )
            second = jnp.concatenate(
                [jnp.where(lane == LANES - 1, ahead, zero), zero, jnp.where(lane == 0, behind, zero)],
                axis=0,
            )
            return [first.astype(BF16), second.astype(BF16)]

        def step(i, c):
            lefts, rights = [], []
            for u in range(group):
                h = i * group + u
                lefts += shifted(h)
                rights.append(wide[pl.ds(aligned(h, chans), 3 * chans), :])
            acc[:, : 3 * chans] += lax.dot_general(
                jnp.concatenate(lefts, axis=1),
                jnp.concatenate(rights, axis=1),
                (((1,), (1,)), ((), ())),
                preferred_element_type=F32,
            )
            return c

        acc[...] = jnp.zeros_like(acc)
        lax.fori_loop(0, rows // group, step, 0)

    take_in(fields_ref, fwide, send_a, 0)
    take_in(cot_ref, gwide, send_a, 1)
    pl.semaphore_wait(barrier, nlon - 1 + nlat - 1 + diagonals)
    start_exchange(0, send_a, recv_a, pole_a)
    rim_weights()
    finish_exchange(0, send_a, recv_a, pole_a)
    ghosts_forward(fwide, recv_a, pole_a, 0)
    ghosts_backward(gwide, recv_a, pole_a, 1)

    root = math.sqrt(2.0 / math.pi)

    def hidden_row(h, packed):
        u = conv_row(w_ref[0], fwide, h)
        square = u * u
        t = jnp.tanh(root * (u + 0.044715 * (square * u)))
        half = 0.5 * (1.0 + t)
        slope[pl.ds(aligned(h, chans), chans), :] = half + (0.5 * root) * u * (1.0 - t * t) * (
            1.0 + (3 * 0.044715) * square
        )
        value = u * half
        hwide[pl.ds(aligned(h + 1, chans), chans), own_rows] = value.astype(BF16)
        return pack_edge(h, value, packed)

    none = jnp.zeros((chans, LANES), F32)
    packed = lax.fori_loop(0, rows, hidden_row, none, unroll=2)
    edges_into(send_b, None, hwide, packed)
    start_exchange(1, send_b, recv_b, pole_b)

    def weights_at(kernel_at, h):
        place = jnp.where(h == 0, 0, jnp.where(h == rows - 1, 2, 1))
        return wedge[kernel_at * 3 + place]

    def back_row(h, packed):
        back = conv_row(weights_at(1, h), gwide, h)
        value = back * slope[pl.ds(aligned(h, chans), chans), :]
        dwide[pl.ds(aligned(h + 1, chans), chans), own_rows] = value.astype(BF16)
        return pack_edge(h, value, packed)

    packed = lax.fori_loop(0, rows, back_row, none, unroll=2)
    edges_into(send_c, None, dwide, packed)
    start_exchange(2, send_c, recv_c, pole_c)

    gradient(dwide, fwide, acc_one)
    finish_exchange(1, send_b, recv_b, pole_b)
    ghosts_forward(hwide, recv_b, pole_b, None)
    gradient(gwide, hwide, acc_two)

    tall = 3 * chans
    tall_lane = lane_index((tall, LANES))
    rs_send[pl.ds(0, tall), :] = acc_one[:, :LANES].astype(BF16)
    rs_send[pl.ds(tall, tall), :] = acc_two[:, :LANES].astype(BF16)
    rs_send[pl.ds(2 * tall, tall), :] = jnp.where(
        tall_lane < chans, acc_one[:, LANES:], pltpu.roll(acc_two[:, LANES:], chans, 1)
    ).astype(BF16)

    def rows_of(k):
        return pl.ds(aligned(k, piece), piece)

    def rs_copy(k):
        return put(
            rs_send.at[rows_of(k)], rs_recv.at[lon], rs_ssem.at[k], rs_rsem.at[lon], lat, k
        )

    def rs_start(k, c):
        @pl.when(k != lon)
        def _():
            rs_copy(k).start()

        return c

    lax.fori_loop(0, owners, rs_start, 0)

    @pl.when(lon < owners)
    def _():
        rs_recv[lon] = rs_send[rows_of(lon), :]

    def out_row(h, c):
        stage[pl.ds(h, chans, stride=rows), :] = conv_row(w_ref[1], hwide, h)
        return c

    lax.fori_loop(0, rows, out_row, 0, unroll=2)
    out_ref[...] = stage[...].astype(BF16)

    def ar_copy(k):
        return put(
            ar_send, ar_recv.at[lat], ar_ssem.at[k], ar_rsem.at[lat], other(k, lat, nlat), lon
        )

    @pl.when(lon < owners)
    def _():
        def wait(k, c):
            source = other(k, lon, nlon)
            put(
                rs_recv.at[lon], rs_recv.at[source], rs_ssem.at[0], rs_rsem.at[source], lat, lon
            ).wait_recv()
            return c

        lax.fori_loop(1, nlon, wait, 0)
        total = rs_recv[0].astype(F32)
        for k in range(1, nlon):
            total = total + rs_recv[k].astype(F32)
        ar_send[...] = total.astype(BF16)
        ar_recv[lat] = total.astype(BF16)

        def start(k, c):
            ar_copy(k).start()
            return c

        lax.fori_loop(1, nlat, start, 0)

    def rs_wait(k, c):
        @pl.when(k != lon)
        def _():
            rs_copy(k).wait_send()

        return c

    lax.fori_loop(0, owners, rs_wait, 0)

    finish_exchange(2, send_c, recv_c, pole_c)
    ghosts_backward(dwide, recv_c, pole_c, None)

    def df_row(h, c):
        stage[pl.ds(h, chans, stride=rows), :] = conv_row(weights_at(0, h), dwide, h)
        return c

    lax.fori_loop(0, rows, df_row, 0, unroll=2)
    df_ref[...] = stage[...].astype(BF16)

    def ag_copy(k):
        return put(
            ag_buf.at[rows_of(lon)], ag_buf.at[rows_of(lon)], ag_ssem.at[k], ag_rsem.at[lon],
            lat, other(k, lon, nlon),
        )

    @pl.when(lon < owners)
    def _():
        def wait(k, c):
            source = other(k, lat, nlat)
            ar_copy(k).wait_send()
            put(
                ar_send, ar_recv.at[source], ar_ssem.at[k], ar_rsem.at[source], lat, lon
            ).wait_recv()
            return c

        lax.fori_loop(1, nlat, wait, 0)
        total = ar_recv[0].astype(F32)
        for k in range(1, nlat):
            total = total + ar_recv[k].astype(F32)
        ag_buf[rows_of(lon), :] = total.astype(BF16)

        def start(k, c):
            ag_copy(k).start()
            return c

        lax.fori_loop(1, nlon, start, 0)

    def ag_wait(k, c):
        @pl.when(k != lon)
        def _():
            put(
                ag_buf.at[rows_of(k)], ag_buf.at[rows_of(k)], ag_ssem.at[0], ag_rsem.at[k],
                lat, lon,
            ).wait_recv()

        return c

    lax.fori_loop(0, owners, ag_wait, 0)

    @pl.when(lon < owners)
    def _():
        def wait(k, c):
            ag_copy(k).wait_send()
            return c

        lax.fori_loop(1, nlon, wait, 0)

    last = ag_buf[pl.ds(2 * tall, tall), :].astype(F32) * scale
    last_turned = pltpu.roll(last, chans, 1)
    for which, ref in ((0, g1_ref), (1, g2_ref)):
        block = ag_buf[pl.ds(which * tall, tall), :].astype(F32) * scale
        turned_block = pltpu.roll(block, chans, 1)
        for s in range(3):
            cut = slice(s * chans, (s + 1) * chans)
            ref[0, s] = block[cut, :chans]
            ref[1, s] = turned_block[cut, :chans]
            ref[2, s] = (last if which == 0 else last_turned)[cut, :chans]


def on_device(
    nlon, nlat, fields_in, weight_one, weight_two, cotangent,
    north_map, north_code, south_map, south_code,
):
    chans, rows, cols = fields_in.shape
    scale = 1.0 / math.sqrt(float(rows * cols * nlon * nlat))
    tall = 3 * chans

    def forward_form(w):
        return jnp.transpose(w, (1, 2, 0, 3)).reshape(tall, tall)

    def backward_form(w):
        return jnp.transpose(w[::-1, ::-1], (1, 3, 0, 2)).reshape(tall, tall)

    weights = jnp.stack(
        [
            forward_form(weight_one), forward_form(weight_two),
            backward_form(weight_one), backward_form(weight_two),
        ]
    )
    total_rows = 3 * tall
    owners = max(k for k in range(1, nlon + 1) if total_rows % (16 * k) == 0)
    piece = total_rows // owners
    vmem = pl.BlockSpec(memory_space=pltpu.VMEM)
    smem = pl.BlockSpec(memory_space=pltpu.SMEM)
    wide = pltpu.VMEM(((rows + 2) * chans, 2 * LANES), BF16)
    edge = (chans, LANES)
    dma = pltpu.SemaphoreType.DMA
    scratch = [
        pltpu.VMEM((chans * rows, LANES), F32), wide, wide, wide, wide,
        pltpu.VMEM((chans * rows, LANES), F32),
        pltpu.VMEM((6, tall, tall), BF16),
        pltpu.VMEM((3, 2) + edge, BF16), pltpu.VMEM((8, 2) + edge, BF16),
        pltpu.VMEM((nlon, 2) + edge, BF16),
        pltpu.VMEM((3,) + edge, BF16), pltpu.VMEM((8,) + edge, BF16),
        pltpu.VMEM((nlon,) + edge, BF16),
        pltpu.VMEM((3,) + edge, BF16), pltpu.VMEM((8,) + edge, BF16),
        pltpu.VMEM((nlon,) + edge, BF16),
        pltpu.VMEM((tall, 2 * LANES), F32), pltpu.VMEM((tall, 2 * LANES), F32),
        pltpu.VMEM((total_rows, LANES), BF16), pltpu.VMEM((nlon, piece, LANES), BF16),
        pltpu.VMEM((piece, LANES), BF16), pltpu.VMEM((nlat, piece, LANES), BF16),
        pltpu.VMEM((total_rows, LANES), BF16),
        dma((3, 8)), dma((3, 8)), dma((3, nlon)), dma((3, nlon)),
        dma((nlon,)), dma((nlon,)), dma((nlat,)), dma((nlat,)), dma((nlon,)), dma((nlon,)),
    ]
    output, d_fields, grad_one, grad_two = pl.pallas_call(
        functools.partial(kernel, nlon, nlat, rows, chans, owners, scale),
        out_shape=(
            jax.ShapeDtypeStruct((chans * rows, cols), BF16),
            jax.ShapeDtypeStruct((chans * rows, cols), BF16),
            jax.ShapeDtypeStruct((3, 3, chans, chans), F32),
            jax.ShapeDtypeStruct((3, 3, chans, chans), F32),
        ),
        in_specs=[vmem, vmem, vmem, smem, smem, smem, smem],
        out_specs=(vmem, vmem, vmem, vmem),
        scratch_shapes=scratch,
        compiler_params=pltpu.CompilerParams(
            collective_id=0, has_side_effects=True, vmem_limit_bytes=48 * 1024 * 1024
        ),
    )(
        fields_in.reshape(chans * rows, cols), cotangent.reshape(chans * rows, cols), weights,
        north_map, north_code, south_map, south_code,
    )
    shape = (chans, rows, cols)
    return (output.reshape(shape), d_fields.reshape(shape), grad_one, grad_two)


def solution(mesh):
    placed = (P(None, "lat", "lon"), P(), P(), P(None, "lat", "lon"), P(), P(), P(), P())
    return jax.shard_map(
        functools.partial(on_device, mesh.shape["lon"], mesh.shape["lat"]),
        mesh=mesh,
        in_specs=placed,
        out_specs=(P(None, "lat", "lon"), P(None, "lat", "lon"), P(), P()),
        check_vma=False,
    )
```

time: 523 us -> 70.8 us (0.14); the launches traced: 513 us -> 70.7 us
  waiting for transfers between devices: 259 us -> 0 us
  local copies, waits for them, and re-layouts: 89.5 us -> 7.58 us
  blocking collectives: 77.7 us -> 0 us
  Pallas kernels: 0 us -> 62.3 us
  starting transfers between devices: 32.6 us -> 0 us
  other arithmetic: 20.8 us -> 0.09 us
  matrix products: 17.7 us -> 0 us
  between operations: 15.4 us -> 0.75 us
    psum x1 -> x0, waiting for transfers between devices: 258 us -> none  [on_device(): summed_one, summed_two = lax.psum((local_one, local_two), ('lon', 'lat'))]
    all_gather x4 -> x0, blocking collectives: 77.7 us -> none  [the longest x2 40.3 us: fold_back(): rim_rows = lax.all_gather(rim_row[None], 'lon', axis=0, tiled=True)]
    pallas_call x0 -> x1, Pallas kernels: none -> 62.3 us  [on_device(): pl.pallas_call(functools.partial(kernel, nlon, nlat, rows, chans, owners,...]
    ppermute x16 -> x0, starting transfers between devices: 32.5 us -> none  [the longest x4 12 us: shifted_2(): return lax.ppermute(x, axis, pairs)]
    scatter-add x4 -> x0, local copies, waits for them, and re-layouts: 28.2 us -> none  [the longest x2 16.7 us: fold_back(): inner_part = inner_part.at[:, :, -1].add(from_east)]
    unnamed x78 -> x20, local copies, waits for them, and re-layouts: 33.5 us -> 5.4 us
    conv_general_dilated x4 -> x0, matrix products: 9.27 us -> none  [the longest x2 5.6 us: convolve(): lax.conv_general_dilated(padded[None], weight, (1, 1), 'VALID', dimension...]
    slice x8 -> x0, local copies, waits for them, and re-layouts: 9.14 us -> none  [the longest x2 2.77 us: fold_back(): inner_part = d_pad[:, :, 1:-1]]
  transfers between devices with their start and end apart: 17 -> 0, of which waited for: 2 -> 0; matrix products, arithmetic and copies ran while one was open for 21% -> 0% of each run, Pallas kernels for 0% -> 0%
where the time goes in v1:
time: 70.8 us; the launch traced here: 70.7 us
  Pallas kernels  62.3 us (88%)
  local copies, waits for them, and re-layouts  7.58 us (11%)
  between operations  0.75 us (1%)
    pallas_call x1, Pallas kernels, on_device(): pl.pallas_call(functools.partial(kernel, nlon, nlat, rows, chans, owners,...  62.3 us
    unnamed x20, local copies, waits for them, and re-layouts  5.4 us

profile of v1, /device:TPU:1, one launch (start us, length us, event | category | flops | bytes accessed | tf_op | source)
XLA Modules:
  0.0 70.7 jit_solution(1522381515307678547)
XLA Ops:
  0.6 0.9 %reverse_bitcast_fusion.1 = bf16[3,64,3,64]{1,3,0,2:T(8,128)(2,1)S(1)} fusion(bf16[3,3,64,64]{3,2,1,0:T(8,128)(2,1)} %param.9), kind=kLoop, calls=%fused_computation.2 | loop fusion | bytes 147456 | tf_op jit(solution)/shard_map/transpose | solution.py:581
  1.6 0.2 copy.18
  1.7 0.0 copy-start.6
  1.7 0.2 stack_reshape.14
  1.9 0.7 %copy-done.6 = bf16[3,3,64,64]{3,2,1,0:T(8,128)(2,1)S(1)} copy-done((bf16[3,3,64,64]{3,2,1,0:T(8,128)(2,1)S(1)}, bf16[3,3,64,64]{3,2,1,0:T(8,128)(2,1)}, u32[]{:S(2)}) %copy-start.6) | copy-done | bytes 73752
  2.7 0.2 copy.19
  2.8 0.2 stack_reshape.15
  3.0 0.1 copy.17
  3.1 0.0 copy-start.7
  3.1 0.2 stack_reshape.13
  3.3 0.7 %copy-done.7 = bf16[3,3,64,64]{3,2,1,0:T(8,128)(2,1)S(1)} copy-done((bf16[3,3,64,64]{3,2,1,0:T(8,128)(2,1)S(1)}, bf16[3,3,64,64]{3,2,1,0:T(8,128)(2,1)}, u32[]{:S(2)}) %copy-start.7) | copy-done | bytes 73752
  4.0 0.1 copy.16
  4.2 0.0 copy-start
  4.2 0.0 copy-start.1
  4.2 0.2 stack_reshape.12
  4.4 0.0 copy-start.2
  4.4 0.0 copy-start.3
  4.4 0.0 copy-start.4
  4.4 0.0 copy-start.5
  4.4 0.1 pad_maximum_fusion.w_ref
  4.5 0.7 %copy-done = bf16[64,32,128]{2,1,0:T(8,128)(2,1)S(1)} copy-done((bf16[64,32,128]{2,1,0:T(8,128)(2,1)S(1)}, bf16[64,32,128]{2,1,0:T(8,128)(2,1)}, u32[]{:S(2)}) %copy-start) | copy-done | bytes 524312
  5.2 0.2 copy-done.1
  5.4 0.0 copy-done.2
  5.4 0.0 copy-done.3
  5.4 0.0 copy-done.4
  5.4 0.0 copy-done.5
  5.4 62.3 %shard_map.111 = (bf16[2048,128]{1,0:T(8,128)(2,1)S(1)}, bf16[2048,128]{1,0:T(8,128)(2,1)S(1)}, f32[3,3,64,64]{3,2,1,0:T(8,128)S(1)}, f32[3,3,64,64]{3,2,1,0:T(8,128)S(1)}) custom-call(bf16[2048,128]{1,0:T(8,128)(2,1)S(1)} %bitcast.10, bf16[2048,128]{1,0:T(8,128)(2,1)S(1)} %bitcast.11, bf16[4,192,192]{2,1,0:T(8,128)(2,1)S(1)} %pad_maximum_fusion.w_ref, ...), custom_call_target="tpu_custom_call" | custom-call | tf_op jit(solution)/shard_map/pallas_call | solution.py:614
  67.7 0.8 %copy.24 = bf16[64,32,128]{2,1,0:T(8,128)(2,1)} copy(bf16[64,32,128]{2,1,0:T(8,128)(2,1)S(1)} %bitcast.13) | data formatting | bytes 1048576
  68.5 0.8 %copy.25 = bf16[64,32,128]{2,1,0:T(8,128)(2,1)} copy(bf16[64,32,128]{2,1,0:T(8,128)(2,1)S(1)} %bitcast.12) | data formatting | bytes 1048576
  69.3 0.7 %copy.26 = f32[3,3,64,64]{3,2,1,0:T(8,128)} copy(f32[3,3,64,64]{3,2,1,0:T(8,128)S(1)} %get-tuple-element.18) | data formatting | bytes 294912
  70.0 0.7 %copy.27 = f32[3,3,64,64]{3,2,1,0:T(8,128)} copy(f32[3,3,64,64]{3,2,1,0:T(8,128)S(1)} %get-tuple-element.19) | data formatting | bytes 294912
  (1 shorter events, 0.0 us)
Async XLA Ops:
  1.7 0.9 %copy-start.6 = (bf16[3,3,64,64]{3,2,1,0:T(8,128)(2,1)S(1)}, bf16[3,3,64,64]{3,2,1,0:T(8,128)(2,1)}, u32[]{:S(2)}) copy-start(bf16[3,3,64,64]{3,2,1,0:T(8,128)(2,1)} %param.10) | copy-start | bytes 221188
  3.1 0.9 %copy-start.7 = (bf16[3,3,64,64]{3,2,1,0:T(8,128)(2,1)S(1)}, bf16[3,3,64,64]{3,2,1,0:T(8,128)(2,1)}, u32[]{:S(2)}) copy-start(bf16[3,3,64,64]{3,2,1,0:T(8,128)(2,1)} %param.9) | copy-start | bytes 221188
  4.2 1.0 %copy-start = (bf16[64,32,128]{2,1,0:T(8,128)(2,1)S(1)}, bf16[64,32,128]{2,1,0:T(8,128)(2,1)}, u32[]{:S(2)}) copy-start(bf16[64,32,128]{2,1,0:T(8,128)(2,1)} %param.8) | copy-start | bytes 1572868
  4.2 1.2 %copy-start.1 = (bf16[64,32,128]{2,1,0:T(8,128)(2,1)S(1)}, bf16[64,32,128]{2,1,0:T(8,128)(2,1)}, u32[]{:S(2)}) copy-start(bf16[64,32,128]{2,1,0:T(8,128)(2,1)} %param.11) | copy-start | bytes 1572868
  4.4 1.0 %copy-start.2 = (s32[16]{0:T(128)S(1)}, s32[16]{0:T(128)}, u32[]{:S(2)}) copy-start(s32[16]{0:T(128)} %north_map.1) | copy-start | bytes 196
  4.4 1.0 %copy-start.3 = (s32[16]{0:T(128)S(1)}, s32[16]{0:T(128)}, u32[]{:S(2)}) copy-start(s32[16]{0:T(128)} %north_code.1) | copy-start | bytes 196
  4.4 1.0 %copy-start.4 = (s32[16]{0:T(128)S(1)}, s32[16]{0:T(128)}, u32[]{:S(2)}) copy-start(s32[16]{0:T(128)} %south_map.1) | copy-start | bytes 196
  4.4 1.0 %copy-start.5 = (s32[16]{0:T(128)S(1)}, s32[16]{0:T(128)}, u32[]{:S(2)}) copy-start(s32[16]{0:T(128)} %south_code.1) | copy-start | bytes 196

commit v2 on v1

--- a/solution.py
+++ b/solution.py
@@ -24,9 +24,9 @@
 
 def kernel(
     nlon, nlat, rows, chans, owners, scale,
-    fields_ref, cot_ref, w_ref, north_map, north_code, south_map, south_code,
+    fields_ref, cot_ref, one_ref, two_ref, north_map, north_code, south_map, south_code,
     out_ref, df_ref, g1_ref, g2_ref,
-    stage, fwide, gwide, hwide, dwide, slope, wedge,
+    stage, stage_two, fwide, gwide, hwide, dwide, slope, w_ref, wedge,
     send_a, recv_a, pole_a, send_b, recv_b, pole_b, send_c, recv_c, pole_c,
     acc_one, acc_two, rs_send, rs_recv, ar_send, ar_recv, ag_buf,
     near_send, near_recv, pole_send, pole_recv,
@@ -186,12 +186,11 @@
     def code_at(k):
         return jnp.where(at_top, north_code[k], south_code[k])
 
-    def owner_of_copy():
-        def step(k, c):
-            hit = map_at(k) == lon
-            return jnp.where(hit, k, c[0]), jnp.where(hit, code_at(k), c[1])
-
-        return lax.fori_loop(0, nlon, step, (jnp.int32(0), jnp.int32(0)))
+    def find_owner(k, c):
+        hit = map_at(k) == lon
+        return jnp.where(hit, k, c[0]), jnp.where(hit, code_at(k), c[1])
+
+    rim_source, rim_code = lax.fori_loop(0, nlon, find_owner, (jnp.int32(0), jnp.int32(0)))
 
     def turned(row, code):
         i = lax.broadcasted_iota(jnp.int32, (LANES, LANES), 0)
@@ -217,7 +216,7 @@
             )
             return c
 
-        lax.fori_loop(0, rows, step, 0, unroll=4)
+        lax.fori_loop(0, rows, step, 0, unroll=32)
 
     def edges_into(send, part, wide, packed):
         top, bottom, side = (
@@ -231,7 +230,7 @@
         keep = jnp.logical_or(lane == 2 * h, lane == lax.rem(2 * h + LANES - 1, LANES))
         return jnp.where(keep, pltpu.roll(value, 2 * h, 1), packed)
 
-    def take_in(source, wide, send, part):
+    def take_in(source, stage, wide, send, part):
         stage[...] = source[...].astype(F32)
 
         def step(h, packed):
@@ -239,7 +238,7 @@
             wide[pl.ds(aligned(h + 1, chans), chans), own_rows] = value.astype(BF16)
             return pack_edge(h, value, packed)
 
-        packed = lax.fori_loop(0, rows, step, jnp.zeros((chans, LANES), F32), unroll=4)
+        packed = lax.fori_loop(0, rows, step, jnp.zeros((chans, LANES), F32), unroll=32)
         edges_into(send, part, wide, packed)
 
     def ghosts_forward(wide, recv, pole, part):
@@ -274,14 +273,12 @@
             return recv[slot] if part is None else recv[slot, part]
 
         def rim(row):
-            source, code = owner_of_copy()
-
             def strip(shift):
-                index = lax.rem(source + shift + nlon, nlon)
-                return turned(pole[index] if part is None else pole[index, part], code)
+                index = lax.rem(rim_source + shift + nlon, nlon)
+                return turned(pole[index] if part is None else pole[index, part], rim_code)
 
             before, mid, after = strip(-1), strip(0), strip(1)
-            flip = code == 1
+            flip = rim_code == 1
             set_ghost_row(
                 wide, row, jnp.where(flip, after, before), mid, jnp.where(flip, before, after)
             )
@@ -303,6 +300,34 @@
         @pl.when(at_bottom)
         def _():
             rim(rows + 1)
+
+    def weight_forms():
+        def spot(shape, shift):
+            i = lax.broadcasted_iota(jnp.int32, shape, 0)
+            j = lax.broadcasted_iota(jnp.int32, shape, 1)
+            return jnp.where(i + shift == j, 1.0, 0.0).astype(BF16)
+
+        tall = 3 * chans
+        for at, ref in ((0, one_ref), (1, two_ref)):
+            total = jnp.zeros((tall, tall), F32)
+            for r in range(3):
+                total = total + jnp.dot(
+                    ref[r * tall : (r + 1) * tall, :],
+                    spot((chans, tall), r * chans),
+                    preferred_element_type=F32,
+                )
+            w_ref[at] = total.astype(BF16)
+            for s in range(3):
+                blocks = [
+                    ref[((2 - r) * 3 + 2 - s) * chans : ((2 - r) * 3 + 3 - s) * chans, :]
+                    for r in range(3)
+                ]
+                w_ref[2 + at, s * chans : (s + 1) * chans, :] = lax.dot_general(
+                    spot((chans, chans), 0),
+                    jnp.concatenate(blocks, axis=0),
+                    (((1,), (1,)), ((), ())),
+                    preferred_element_type=F32,
+                ).astype(BF16)
 
     def rim_weights():
         for kernel_at in range(2):
@@ -311,7 +336,6 @@
                 wedge[kernel_at * 3 + place] = base
 
             def replace(place, into, out_of):
-                _, code = owner_of_copy()
                 full = base.astype(F32)
                 shown = lax.broadcasted_iota(jnp.int32, full.shape, 1) // chans == into
                 width = full.shape[1]
@@ -322,7 +346,7 @@
                 swapped = jnp.concatenate(
                     [moved[2 * chans :], moved[chans : 2 * chans], moved[:chans]], axis=0
                 )
-                chosen = jnp.where(code == 1, swapped, moved)
+                chosen = jnp.where(rim_code == 1, swapped, moved)
                 wedge[kernel_at * 3 + place] = jnp.where(shown, chosen, full).astype(BF16)
 
             @pl.when(at_top)
@@ -343,7 +367,7 @@
         )
 
     def gradient(up_wide, wide, acc):
-        group = 4
+        group = 16
 
         def shifted(h):
             g = up_wide[pl.ds(aligned(h + 1, chans), chans), own_rows].astype(F32)
@@ -377,10 +401,11 @@
         acc[...] = jnp.zeros_like(acc)
         lax.fori_loop(0, rows // group, step, 0)
 
-    take_in(fields_ref, fwide, send_a, 0)
-    take_in(cot_ref, gwide, send_a, 1)
+    take_in(fields_ref, stage, fwide, send_a, 0)
+    take_in(cot_ref, stage_two, gwide, send_a, 1)
     pl.semaphore_wait(barrier, nlon - 1 + nlat - 1 + diagonals)
     start_exchange(0, send_a, recv_a, pole_a)
+    weight_forms()
     rim_weights()
     finish_exchange(0, send_a, recv_a, pole_a)
     ghosts_forward(fwide, recv_a, pole_a, 0)
@@ -401,7 +426,7 @@
         return pack_edge(h, value, packed)
 
     none = jnp.zeros((chans, LANES), F32)
-    packed = lax.fori_loop(0, rows, hidden_row, none, unroll=2)
+    packed = lax.fori_loop(0, rows, hidden_row, none, unroll=32)
     edges_into(send_b, None, hwide, packed)
     start_exchange(1, send_b, recv_b, pole_b)
 
@@ -415,7 +440,7 @@
         dwide[pl.ds(aligned(h + 1, chans), chans), own_rows] = value.astype(BF16)
         return pack_edge(h, value, packed)
 
-    packed = lax.fori_loop(0, rows, back_row, none, unroll=2)
+    packed = lax.fori_loop(0, rows, back_row, none, unroll=32)
     edges_into(send_c, None, dwide, packed)
     start_exchange(2, send_c, recv_c, pole_c)
 
@@ -457,7 +482,7 @@
         stage[pl.ds(h, chans, stride=rows), :] = conv_row(w_ref[1], hwide, h)
         return c
 
-    lax.fori_loop(0, rows, out_row, 0, unroll=2)
+    lax.fori_loop(0, rows, out_row, 0, unroll=32)
     out_ref[...] = stage[...].astype(BF16)
 
     def ar_copy(k):
@@ -503,7 +528,7 @@
         stage[pl.ds(h, chans, stride=rows), :] = conv_row(weights_at(0, h), dwide, h)
         return c
 
-    lax.fori_loop(0, rows, df_row, 0, unroll=2)
+    lax.fori_loop(0, rows, df_row, 0, unroll=32)
     df_ref[...] = stage[...].astype(BF16)
 
     def ag_copy(k):
@@ -573,19 +598,6 @@
     chans, rows, cols = fields_in.shape
     scale = 1.0 / math.sqrt(float(rows * cols * nlon * nlat))
     tall = 3 * chans
-
-    def forward_form(w):
-        return jnp.transpose(w, (1, 2, 0, 3)).reshape(tall, tall)
-
-    def backward_form(w):
-        return jnp.transpose(w[::-1, ::-1], (1, 3, 0, 2)).reshape(tall, tall)
-
-    weights = jnp.stack(
-        [
-            forward_form(weight_one), forward_form(weight_two),
-            backward_form(weight_one), backward_form(weight_two),
-        ]
-    )
     total_rows = 3 * tall
     owners = max(k for k in range(1, nlon + 1) if total_rows % (16 * k) == 0)
     piece = total_rows // owners
@@ -595,8 +607,10 @@
     edge = (chans, LANES)
     dma = pltpu.SemaphoreType.DMA
     scratch = [
-        pltpu.VMEM((chans * rows, LANES), F32), wide, wide, wide, wide,
+        pltpu.VMEM((chans * rows, LANES), F32), pltpu.VMEM((chans * rows, LANES), F32),
+        wide, wide, wide, wide,
         pltpu.VMEM((chans * rows, LANES), F32),
+        pltpu.VMEM((4, tall, tall), BF16),
         pltpu.VMEM((6, tall, tall), BF16),
         pltpu.VMEM((3, 2) + edge, BF16), pltpu.VMEM((8, 2) + edge, BF16),
         pltpu.VMEM((nlon, 2) + edge, BF16),
@@ -619,14 +633,15 @@
             jax.ShapeDtypeStruct((3, 3, chans, chans), F32),
             jax.ShapeDtypeStruct((3, 3, chans, chans), F32),
         ),
-        in_specs=[vmem, vmem, vmem, smem, smem, smem, smem],
+        in_specs=[vmem, vmem, vmem, vmem, smem, smem, smem, smem],
         out_specs=(vmem, vmem, vmem, vmem),
         scratch_shapes=scratch,
         compiler_params=pltpu.CompilerParams(
             collective_id=0, has_side_effects=True, vmem_limit_bytes=48 * 1024 * 1024
         ),
     )(
-        fields_in.reshape(chans * rows, cols), cotangent.reshape(chans * rows, cols), weights,
+        fields_in.reshape(chans * rows, cols), cotangent.reshape(chans * rows, cols),
+        weight_one.reshape(9 * chans, chans), weight_two.reshape(9 * chans, chans),
         north_map, north_code, south_map, south_code,
     )
     shape = (chans, rows, cols)

time: 70.8 us -> 58.5 us (0.83)
  Pallas kernels: 62.3 us -> 50 us
    pallas_call x1, Pallas kernels: 62.3 us -> 50 us  [on_device(): pl.pallas_call(functools.partial(kernel, nlon, nlat, rows, chans, owners,...]
    unnamed x20, local copies, waits for them, and re-layouts: 5.4 us -> 7.59 us
    transpose x6 -> x0, local copies, waits for them, and re-layouts: 1.52 us -> none  [the longest x4 1.26 us: backward_form(): return jnp.transpose(w[::-1, ::-1], (1, 3, 0, 2)).reshape(tall, tall)]
where the time goes in v2:
time: 58.5 us; the launch traced here: 58.3 us
  Pallas kernels  50 us (85%)
  local copies, waits for them, and re-layouts  7.59 us (13%)
  between operations  0.68 us (1%)
    pallas_call x1, Pallas kernels, on_device(): pl.pallas_call(functools.partial(kernel, nlon, nlat, rows, chans, owners,...  50 us
    unnamed x20, local copies, waits for them, and re-layouts  7.59 us

profile of v2, /device:TPU:1, one launch (start us, length us, event | category | flops | bytes accessed | tf_op | source)
XLA Modules:
  0.0 58.3 jit_solution(17553749328347034241)
XLA Ops:
  0.6 0.0 copy-start.7
  0.6 0.0 copy-start.4
  0.7 0.0 copy-start.5
  0.7 0.0 copy-start.6
  0.7 0.6 %copy-done.7 = s32[16]{0:T(128)S(1)} copy-done((s32[16]{0:T(128)S(1)}, s32[16]{0:T(128)}, u32[]{:S(2)}) %copy-start.7) | copy-done | bytes 88
  1.3 0.0 copy-done.4
  1.3 0.0 copy-done.5
  1.3 0.0 copy-done.6
  1.3 0.0 copy-start
  1.3 1.0 %copy-done = bf16[64,32,128]{2,1,0:T(8,128)(2,1)S(1)} copy-done((bf16[64,32,128]{2,1,0:T(8,128)(2,1)S(1)}, bf16[64,32,128]{2,1,0:T(8,128)(2,1)}, u32[]{:S(2)}) %copy-start) | copy-done | bytes 524312
  2.4 0.0 copy-start.1
  2.4 1.0 %copy-done.1 = bf16[64,32,128]{2,1,0:T(8,128)(2,1)S(1)} copy-done((bf16[64,32,128]{2,1,0:T(8,128)(2,1)S(1)}, bf16[64,32,128]{2,1,0:T(8,128)(2,1)}, u32[]{:S(2)}) %copy-start.1) | copy-done | bytes 524312
  3.4 0.0 copy-start.2
  3.4 0.9 %copy-done.2 = bf16[3,3,64,64]{3,2,1,0:T(8,128)(2,1)S(1)} copy-done((bf16[3,3,64,64]{3,2,1,0:T(8,128)(2,1)S(1)}, bf16[3,3,64,64]{3,2,1,0:T(8,128)(2,1)}, u32[]{:S(2)}) %copy-start.2) | copy-done | bytes 73752
  4.3 0.0 copy-start.3
  4.3 0.9 %copy-done.3 = bf16[3,3,64,64]{3,2,1,0:T(8,128)(2,1)S(1)} copy-done((bf16[3,3,64,64]{3,2,1,0:T(8,128)(2,1)S(1)}, bf16[3,3,64,64]{3,2,1,0:T(8,128)(2,1)}, u32[]{:S(2)}) %copy-start.3) | copy-done | bytes 73752
  5.2 50.0 %shard_map.111 = (bf16[2048,128]{1,0:T(8,128)(2,1)S(1)}, bf16[2048,128]{1,0:T(8,128)(2,1)S(1)}, f32[3,3,64,64]{3,2,1,0:T(8,128)S(1)}, f32[3,3,64,64]{3,2,1,0:T(8,128)S(1)}) custom-call(bf16[2048,128]{1,0:T(8,128)(2,1)S(1)} %bitcast.6, bf16[2048,128]{1,0:T(8,128)(2,1)S(1)} %bitcast.7, bf16[576,64]{1,0:T(8,128)(2,1)S(1)} %bitcast.10, ...), custom_call_target="tpu_custom_call" | custom-call | tf_op jit(solution)/shard_map/pallas_call | solution.py:628
  55.3 0.8 %copy.16 = bf16[64,32,128]{2,1,0:T(8,128)(2,1)} copy(bf16[64,32,128]{2,1,0:T(8,128)(2,1)S(1)} %bitcast.9) | data formatting | bytes 1048576
  56.1 0.8 %copy.17 = bf16[64,32,128]{2,1,0:T(8,128)(2,1)} copy(bf16[64,32,128]{2,1,0:T(8,128)(2,1)S(1)} %bitcast.8) | data formatting | bytes 1048576
  56.8 0.7 %copy.18 = f32[3,3,64,64]{3,2,1,0:T(8,128)} copy(f32[3,3,64,64]{3,2,1,0:T(8,128)S(1)} %get-tuple-element.18) | data formatting | bytes 294912
  57.6 0.7 %copy.19 = f32[3,3,64,64]{3,2,1,0:T(8,128)} copy(f32[3,3,64,64]{3,2,1,0:T(8,128)S(1)} %get-tuple-element.19) | data formatting | bytes 294912
Async XLA Ops:
  0.6 0.7 %copy-start.7 = (s32[16]{0:T(128)S(1)}, s32[16]{0:T(128)}, u32[]{:S(2)}) copy-start(s32[16]{0:T(128)} %south_code.1) | copy-start | bytes 196
  0.6 0.7 %copy-start.4 = (s32[16]{0:T(128)S(1)}, s32[16]{0:T(128)}, u32[]{:S(2)}) copy-start(s32[16]{0:T(128)} %north_map.1) | copy-start | bytes 196
  0.7 0.7 %copy-start.5 = (s32[16]{0:T(128)S(1)}, s32[16]{0:T(128)}, u32[]{:S(2)}) copy-start(s32[16]{0:T(128)} %north_code.1) | copy-start | bytes 196
  0.7 0.7 %copy-start.6 = (s32[16]{0:T(128)S(1)}, s32[16]{0:T(128)}, u32[]{:S(2)}) copy-start(s32[16]{0:T(128)} %south_map.1) | copy-start | bytes 196
  1.3 1.0 %copy-start = (bf16[64,32,128]{2,1,0:T(8,128)(2,1)S(1)}, bf16[64,32,128]{2,1,0:T(8,128)(2,1)}, u32[]{:S(2)}) copy-start(bf16[64,32,128]{2,1,0:T(8,128)(2,1)} %param.8) | copy-start | bytes 1572868
  2.4 1.0 %copy-start.1 = (bf16[64,32,128]{2,1,0:T(8,128)(2,1)S(1)}, bf16[64,32,128]{2,1,0:T(8,128)(2,1)}, u32[]{:S(2)}) copy-start(bf16[64,32,128]{2,1,0:T(8,128)(2,1)} %param.11) | copy-start | bytes 1572868
  3.4 0.9 %copy-start.2 = (bf16[3,3,64,64]{3,2,1,0:T(8,128)(2,1)S(1)}, bf16[3,3,64,64]{3,2,1,0:T(8,128)(2,1)}, u32[]{:S(2)}) copy-start(bf16[3,3,64,64]{3,2,1,0:T(8,128)(2,1)} %param.9) | copy-start | bytes 221188
  4.3 0.9 %copy-start.3 = (bf16[3,3,64,64]{3,2,1,0:T(8,128)(2,1)S(1)}, bf16[3,3,64,64]{3,2,1,0:T(8,128)(2,1)}, u32[]{:S(2)}) copy-start(bf16[3,3,64,64]{3,2,1,0:T(8,128)(2,1)} %param.10) | copy-start | bytes 221188

commit v3 on v2

v3 whole, which is shorter than its diff:
```python
import functools
import math

import jax
import jax.numpy as jnp
from jax import lax
from jax.experimental import pallas as pl
from jax.experimental.pallas import tpu as pltpu
from jax.sharding import PartitionSpec as P

MESH = pl.DeviceIdType.MESH
LANES = 128
F32 = jnp.float32
BF16 = jnp.bfloat16
NT = (((1,), (1,)), ((), ()))
FIELDS, COT, HIDDEN, DPRE = range(4)


def aligned(start, step):
    return pl.multiple_of(start * step, step)


def kernel(
    nlon, nlat, planes, rows, chans, owners, scale,
    fields_hbm, cot_hbm, one_hbm, two_hbm, north_map, north_code, south_map, south_code,
    out_hbm, df_hbm, g1_ref, g2_ref,
    fields_in, cot_in, one_ref, two_ref, out_buf, df_buf,
    stage, stage_two, fwide, gwide, hwide, dwide, slope, w_ref, wedge, rim_row,
    send, recv, pole_f, pole_c, pole_h, pole_d, acc_one, acc_two, sums,
    rs_send, rs_recv, ar_send, ar_recv, ag_buf,
    local_sem, near_send, near_recv, pole_send, pole_recv,
    rs_ssem, rs_rsem, ar_ssem, ar_rsem, ag_ssem, ag_rsem,
):
    lon = lax.axis_index("lon")
    lat = lax.axis_index("lat")
    depth = nlat // planes
    plane = lax.div(lat, depth)
    z = lax.rem(lat, depth)
    group = nlon * planes
    mine = lon + nlon * plane
    west = lax.rem(lon + nlon - 1, nlon)
    east = lax.rem(lon + 1, nlon)
    has_north = lat > 0
    has_south = lat < nlat - 1
    at_top = lat == 0
    at_bottom = lat == nlat - 1
    at_pole = jnp.logical_or(at_top, at_bottom)
    tall = 3 * chans
    lane = lax.broadcasted_iota(jnp.int32, (chans, LANES), 1)
    own = pl.ds(0, LANES)
    ghost_cols = pl.ds(LANES, LANES)
    piece = 3 * tall // owners

    def in_group(g):
        return lax.div(g, nlon) * depth + z, lax.rem(g, nlon)

    def group_peer(k):
        return lax.rem(mine + k, group)

    def along_z(k):
        return plane * depth + lax.rem(z + k, depth), lon

    spread_owners = group % 4 == 0 and owners == group // 4 * 3

    def owner_at(j):
        return lax.div(j, 3) * 4 + lax.rem(j, 3) if spread_owners else j

    if spread_owners:
        owns = lax.rem(mine, 4) < 3
        own_piece = lax.div(mine, 4) * 3 + lax.rem(mine, 4)
    else:
        owns = mine < owners
        own_piece = mine

    barrier = pltpu.get_barrier_semaphore()

    def greet(place):
        pl.semaphore_signal(
            barrier, inc=1, device_id={"lat": place[0], "lon": place[1]}, device_id_type=MESH
        )

    def greet_group(k, c):
        greet(in_group(group_peer(k)))
        return c

    def greet_z(k, c):
        greet(along_z(k))
        return c

    @pl.when(has_north)
    def _():
        for at in (west, lon, east):
            greet((lat - 1, at))

    @pl.when(has_south)
    def _():
        for at in (west, lon, east):
            greet((lat + 1, at))

    lax.fori_loop(1, group, greet_group, 0)
    lax.fori_loop(1, depth, greet_z, 0)
    beside = 3 * has_north.astype(jnp.int32) + 3 * has_south.astype(jnp.int32)

    loads = [
        pltpu.make_async_copy(source, target, local_sem.at[i])
        for i, (source, target) in enumerate(
            [(fields_hbm, fields_in), (cot_hbm, cot_in), (one_hbm, one_ref), (two_hbm, two_ref)]
        )
    ]
    for load in loads:
        load.start()

    def put(src, dst, ssem, rsem, place):
        return pltpu.make_async_remote_copy(
            src_ref=src, dst_ref=dst, send_sem=ssem, recv_sem=rsem,
            device_id={"lat": place[0], "lon": place[1]}, device_id_type=MESH,
        )

    here = (lat, lon)
    pole = (pole_f, pole_c, pole_h, pole_d)

    def near_copies(x):
        def one(part, slot, at, place):
            return put(
                send.at[x, part], recv.at[x, slot], near_send.at[x, at], near_recv.at[x, slot],
                place,
            )

        sides = [one(2, 1, 0, (lat, west)), one(2, 0, 1, (lat, east))]
        up = [
            one(0, 7, 2, (lat - 1, west)), one(0, 6, 3, (lat - 1, lon)), one(0, 5, 4, (lat - 1, east))
        ]
        down = [
            one(1, 4, 5, (lat + 1, west)), one(1, 3, 6, (lat + 1, lon)), one(1, 2, 7, (lat + 1, east))
        ]
        return sides, up, down

    def pole_copy(x, part, k):
        return put(
            send.at[x, part], pole[x].at[lon], pole_send.at[x, k], pole_recv.at[x, lon],
            (lat, lax.rem(lon + k, nlon)),
        )

    def start_exchange(x):
        sides, up, down = near_copies(x)
        for copy in sides:
            copy.start()

        @pl.when(has_north)
        def _():
            for copy in up:
                copy.start()

        @pl.when(has_south)
        def _():
            for copy in down:
                copy.start()

        def pole_start(part):
            def step(k, c):
                pole_copy(x, part, k).start()
                return c

            lax.fori_loop(1, nlon, step, 0)
            pole[x][lon] = send[x, part]

        @pl.when(at_top)
        def _():
            pole_start(0)

        @pl.when(at_bottom)
        def _():
            pole_start(1)

    def arrived(x, slot):
        put(
            send.at[x, 0], recv.at[x, slot], near_send.at[x, 0], near_recv.at[x, slot], here
        ).wait_recv()

    def wait_rows(x):
        @pl.when(has_north)
        def _():
            for slot in (2, 3, 4):
                arrived(x, slot)

        @pl.when(has_south)
        def _():
            for slot in (5, 6, 7):
                arrived(x, slot)

        @pl.when(at_pole)
        def _():
            def step(k, c):
                source = lax.rem(lon + k, nlon)
                put(
                    send.at[x, 0], pole[x].at[source], pole_send.at[x, k],
                    pole_recv.at[x, source], here,
                ).wait_recv()
                return c

            lax.fori_loop(1, nlon, step, 0)

    def wait_sent(x):
        sides, up, down = near_copies(x)
        for copy in sides:
            copy.wait_send()

        @pl.when(has_north)
        def _():
            for copy in up:
                copy.wait_send()

        @pl.when(has_south)
        def _():
            for copy in down:
                copy.wait_send()

        @pl.when(at_pole)
        def _():
            def step(k, c):
                pole_copy(x, 0, k).wait_send()
                return c

            lax.fori_loop(1, nlon, step, 0)

    def map_at(k):
        return jnp.where(at_top, north_map[k], south_map[k])

    def code_at(k):
        return jnp.where(at_top, north_code[k], south_code[k])

    def find_owner(k, c):
        hit = map_at(k) == lon
        return jnp.where(hit, k, c[0]), jnp.where(hit, code_at(k), c[1])

    rim_source, rim_code = lax.fori_loop(0, nlon, find_owner, (jnp.int32(0), jnp.int32(0)))

    def turned(row, code):
        i = lax.broadcasted_iota(jnp.int32, (LANES, LANES), 0)
        j = lax.broadcasted_iota(jnp.int32, (LANES, LANES), 1)
        match = (i + (2 * code - 1) * j) == (LANES - 1) * code
        turn = jnp.where(match, 1.0, 0.0).astype(BF16)
        return jnp.dot(row, turn, preferred_element_type=F32)

    def set_ghost_row(wide, row, left, mid, right):
        place = pl.ds(row * chans, chans)
        wide[place, own] = mid.astype(BF16)
        wide[place, ghost_cols] = jnp.where(lane == 0, right.astype(F32), left.astype(F32)).astype(
            BF16
        )

    def set_ghost_cols(x, wide):
        arrived(x, 0)
        arrived(x, 1)
        merged = jnp.where(lane % 2 == 0, recv[x, 1].astype(F32), recv[x, 0].astype(F32))

        def step(h, c):
            place = pl.ds(aligned(h + 1, chans), chans)
            wide[place, ghost_cols] = pltpu.roll(merged, lax.rem(LANES - 2 * h, LANES), 1).astype(
                BF16
            )
            return c

        lax.fori_loop(0, rows, step, 0, unroll=rows)

    def pack_edge(h, value, packed):
        keep = jnp.logical_or(lane == 2 * h, lane == lax.rem(2 * h + LANES - 1, LANES))
        return jnp.where(keep, pltpu.roll(value, 2 * h, 1), packed)

    def send_edges(x, wide, packed):
        send[x, 0] = wide[pl.ds(chans, chans), own]
        send[x, 1] = wide[pl.ds(rows * chans, chans), own]
        send[x, 2] = packed.astype(BF16)
        start_exchange(x)

    none = jnp.zeros((chans, LANES), F32)

    def take_in(source, stage, wide):
        stage[...] = source[...].astype(F32)

        def step(h, packed):
            value = stage[pl.ds(h, chans, stride=rows), :]
            wide[pl.ds(aligned(h + 1, chans), chans), own] = value.astype(BF16)
            return pack_edge(h, value, packed)

        return lax.fori_loop(0, rows, step, none, unroll=rows)

    def set_ghost_rows(x, wide, forward):
        wait_rows(x)

        @pl.when(has_north)
        def _():
            set_ghost_row(wide, 0, recv[x, 2], recv[x, 3], recv[x, 4])

        @pl.when(has_south)
        def _():
            set_ghost_row(wide, rows + 1, recv[x, 5], recv[x, 6], recv[x, 7])

        def across(row):
            if forward:
                strips = [turned(pole[x][map_at(k)], code_at(k)) for k in (west, lon, east)]
                set_ghost_row(wide, row, *strips)
                return
            before, mid, after = [
                turned(pole[x][lax.rem(rim_source + shift, nlon)], rim_code)
                for shift in (nlon - 1, 0, 1)
            ]
            flip = rim_code == 1
            set_ghost_row(
                wide, row, jnp.where(flip, after, before), mid, jnp.where(flip, before, after)
            )

        @pl.when(at_top)
        def _():
            across(0)

        @pl.when(at_bottom)
        def _():
            across(rows + 1)

    def weight_forms():
        def spot(shape, shift):
            i = lax.broadcasted_iota(jnp.int32, shape, 0)
            j = lax.broadcasted_iota(jnp.int32, shape, 1)
            return jnp.where(i + shift == j, 1.0, 0.0).astype(BF16)

        for at, ref in ((0, one_ref), (1, two_ref)):
            total = jnp.zeros((tall, tall), F32)
            for r in range(3):
                total = total + jnp.dot(
                    ref[r * tall : (r + 1) * tall, :],
                    spot((chans, tall), r * chans),
                    preferred_element_type=F32,
                )
            w_ref[at] = total.astype(BF16)
            for s in range(3):
                blocks = [
                    ref[((2 - r) * 3 + 2 - s) * chans : ((2 - r) * 3 + 3 - s) * chans, :]
                    for r in range(3)
                ]
                w_ref[2 + at, s * chans : (s + 1) * chans, :] = lax.dot_general(
                    spot((chans, chans), 0),
                    jnp.concatenate(blocks, axis=0),
                    NT,
                    preferred_element_type=F32,
                ).astype(BF16)

    def rim_weights():
        for kernel_at in range(2):
            base = w_ref[2 + kernel_at]
            for place in range(3):
                wedge[kernel_at * 3 + place] = base

            def replace(place, into, out_of):
                full = base.astype(F32)
                shown = lax.broadcasted_iota(jnp.int32, full.shape, 1) // chans == into
                i = lax.broadcasted_iota(jnp.int32, full.shape, 0)
                j = lax.broadcasted_iota(jnp.int32, full.shape, 1)
                move = jnp.where(i - out_of * chans == j - into * chans, 1.0, 0.0).astype(BF16)
                moved = jnp.dot(base, move, preferred_element_type=F32)
                swapped = jnp.concatenate(
                    [moved[2 * chans :], moved[chans : 2 * chans], moved[:chans]], axis=0
                )
                chosen = jnp.where(rim_code == 1, swapped, moved)
                wedge[kernel_at * 3 + place] = jnp.where(shown, chosen, full).astype(BF16)

            @pl.when(at_top)
            def _():
                replace(0, 0, 2)

            @pl.when(at_bottom)
            def _():
                replace(2, 2, 0)

    def conv_row(weights, wide, h):
        window = wide[pl.ds(aligned(h, chans), tall), :]
        y = jnp.dot(weights, window, preferred_element_type=F32)
        left = jnp.where(lane == LANES - 1, y[:chans, LANES:], y[:chans, :LANES])
        right = jnp.where(lane == 0, y[2 * chans :, LANES:], y[2 * chans :, :LANES])
        return (
            pltpu.roll(left, 1, 1) + y[chans : 2 * chans, :LANES] + pltpu.roll(right, LANES - 1, 1)
        )

    def shifted(wide, h):
        g = wide[pl.ds(aligned(h + 1, chans), chans), own].astype(F32)
        ahead = pltpu.roll(g, LANES - 1, 1)
        behind = pltpu.roll(g, 1, 1)
        zero = jnp.zeros_like(g)
        first = jnp.concatenate(
            [jnp.where(lane != LANES - 1, ahead, zero), g, jnp.where(lane != 0, behind, zero)],
            axis=0,
        )
        second = jnp.concatenate(
            [jnp.where(lane == LANES - 1, ahead, zero), zero, jnp.where(lane == 0, behind, zero)],
            axis=0,
        )
        return [first.astype(BF16), second.astype(BF16)]

    def gradient(shift_wide, window_wide, acc, shifted_first):
        count = min(16, rows)

        def step(i, c):
            moved, windows = [], []
            for u in range(count):
                h = i * count + u
                moved += shifted(shift_wide, h)
                windows.append(window_wide[pl.ds(aligned(h, chans), tall), :])
            moved, windows = jnp.concatenate(moved, axis=1), jnp.concatenate(windows, axis=1)
            a, b = (moved, windows) if shifted_first else (windows, moved)
            acc[:, :tall] += lax.dot_general(a, b, NT, preferred_element_type=F32)
            return c

        acc[...] = jnp.zeros_like(acc)
        lax.fori_loop(0, rows // count, step, 0)

    def all_rows(row, x, wide, forward):
        set_ghost_cols(x, wide)
        carry = lax.fori_loop(1, rows - 1, row, none, unroll=rows - 2)
        set_ghost_rows(x, wide, forward)
        return lax.fori_loop(0, 2, lambda k, c: row(k * (rows - 1), c), carry, unroll=2)

    loads[0].wait()
    packed = take_in(fields_in, stage, fwide)
    pl.semaphore_wait(barrier, group - 1 + depth - 1 + beside)
    send_edges(FIELDS, fwide, packed)
    loads[1].wait()
    packed = take_in(cot_in, stage_two, gwide)
    send_edges(COT, gwide, packed)
    loads[2].wait()
    loads[3].wait()
    weight_forms()
    rim_weights()

    root = math.sqrt(2.0 / math.pi)

    def hidden_row(h, packed):
        u = conv_row(w_ref[0], fwide, h)
        square = u * u
        t = jnp.tanh(root * (u + 0.044715 * (square * u)))
        half = 0.5 * (1.0 + t)
        slope[pl.ds(aligned(h, chans), chans), :] = half + (0.5 * root) * u * (1.0 - t * t) * (
            1.0 + (3 * 0.044715) * square
        )
        value = u * half
        hwide[pl.ds(aligned(h + 1, chans), chans), own] = value.astype(BF16)
        return pack_edge(h, value, packed)

    packed = all_rows(hidden_row, FIELDS, fwide, True)
    send_edges(HIDDEN, hwide, packed)

    def weights_at(kernel_at, h):
        place = jnp.where(h == 0, 0, jnp.where(h == rows - 1, 2, 1))
        return wedge[kernel_at * 3 + place]

    def back_row(h, packed):
        back = conv_row(weights_at(1, h), gwide, h)
        value = back * slope[pl.ds(aligned(h, chans), chans), :]
        dwide[pl.ds(aligned(h + 1, chans), chans), own] = value.astype(BF16)
        return pack_edge(h, value, packed)

    packed = all_rows(back_row, COT, gwide, False)
    send_edges(DPRE, dwide, packed)

    gradient(dwide, fwide, acc_one, True)

    def set_aside(row):
        place = pl.ds(row * chans, chans)
        rim_row[...] = gwide[place, :]
        gwide[place, :] = jnp.zeros((chans, 2 * LANES), BF16)

    def credit(h, block):
        first, second = shifted(hwide, h)
        moved = jnp.concatenate([first, second], axis=1).astype(F32)
        swapped = jnp.concatenate(
            [moved[2 * chans :], moved[chans : 2 * chans], moved[:chans]], axis=0
        )
        chosen = jnp.where(rim_code == 1, swapped, moved).astype(BF16)
        acc_two[pl.ds(block * chans, chans), :tall] += lax.dot_general(
            rim_row[...], chosen, NT, preferred_element_type=F32
        )

    @pl.when(at_top)
    def _():
        set_aside(0)

    @pl.when(at_bottom)
    def _():
        set_aside(rows + 1)

    gradient(hwide, gwide, acc_two, False)

    @pl.when(at_top)
    def _():
        credit(0, 2)

    @pl.when(at_bottom)
    def _():
        credit(rows - 1, 0)

    sums[pl.ds(0, tall), :] = acc_one[:, :LANES]
    sums[pl.ds(tall, tall), :] = acc_two[:, :LANES]
    half_lane = lax.broadcasted_iota(jnp.int32, (tall, LANES), 1) < chans
    sums[pl.ds(2 * tall, tall), :] = jnp.where(
        half_lane, acc_one[:, LANES:], pltpu.roll(acc_two[:, LANES:], chans, 1)
    )
    for j in range(owners):
        rs_send[j] = sums[pl.ds(j * piece, piece), :].astype(BF16)

    def rs_copy(j):
        return put(
            rs_send.at[j], rs_recv.at[mine], rs_ssem.at[j], rs_rsem.at[mine], in_group(owner_at(j))
        )

    def rs_start(j, c):
        @pl.when(owner_at(j) != mine)
        def _():
            rs_copy(j).start()

        return c

    lax.fori_loop(0, owners, rs_start, 0)

    @pl.when(owns)
    def _():
        rs_recv[mine] = rs_send[own_piece]

    set_ghost_cols(HIDDEN, hwide)
    set_ghost_rows(HIDDEN, hwide, True)

    def out_row(h, c):
        stage[pl.ds(h, chans, stride=rows), :] = conv_row(w_ref[1], hwide, h)
        return c

    lax.fori_loop(0, rows, out_row, 0, unroll=rows)
    out_buf[...] = stage[...].astype(BF16)
    out_copy = pltpu.make_async_copy(out_buf, out_hbm, local_sem.at[4])
    out_copy.start()

    def ar_copy(k):
        return put(ar_send, ar_recv.at[z], ar_ssem.at[k], ar_rsem.at[z], along_z(k))

    @pl.when(owns)
    def _():
        def wait(k, c):
            source = group_peer(k)
            put(
                rs_recv.at[mine], rs_recv.at[source], rs_ssem.at[0], rs_rsem.at[source], here
            ).wait_recv()
            return c

        lax.fori_loop(1, group, wait, 0)
        total = rs_recv[0].astype(F32)
        for k in range(1, group):
            total = total + rs_recv[k].astype(F32)
        ar_send[...] = total.astype(BF16)
        ar_recv[z] = total.astype(BF16)

        def start(k, c):
            ar_copy(k).start()
            return c

        lax.fori_loop(1, depth, start, 0)

    set_ghost_cols(DPRE, dwide)
    set_ghost_rows(DPRE, dwide, False)

    def df_row(h, c):
        stage_two[pl.ds(h, chans, stride=rows), :] = conv_row(weights_at(0, h), dwide, h)
        return c

    lax.fori_loop(0, rows, df_row, 0, unroll=rows)
    df_buf[...] = stage_two[...].astype(BF16)
    df_copy = pltpu.make_async_copy(df_buf, df_hbm, local_sem.at[5])
    df_copy.start()

    def ag_copy(k):
        return put(
            ag_buf.at[own_piece], ag_buf.at[own_piece], ag_ssem.at[k], ag_rsem.at[own_piece],
            in_group(group_peer(k)),
        )

    @pl.when(owns)
    def _():
        def wait(k, c):
            source = lax.rem(z + k, depth)
            put(ar_send, ar_recv.at[source], ar_ssem.at[k], ar_rsem.at[source], here).wait_recv()
            return c

        lax.fori_loop(1, depth, wait, 0)
        total = ar_recv[0].astype(F32)
        for k in range(1, depth):
            total = total + ar_recv[k].astype(F32)
        ag_buf[own_piece] = total.astype(BF16)

        def start(k, c):
            ag_copy(k).start()
            return c

        lax.fori_loop(1, group, start, 0)

    for x in range(4):
        wait_sent(x)

    def rs_sent(j, c):
        @pl.when(owner_at(j) != mine)
        def _():
            rs_copy(j).wait_send()

        return c

    lax.fori_loop(0, owners, rs_sent, 0)

    @pl.when(owns)
    def _():
        def sent(k, c):
            ar_copy(k).wait_send()
            return c

        lax.fori_loop(1, depth, sent, 0)

    def ag_wait(j, c):
        @pl.when(owner_at(j) != mine)
        def _():
            put(ag_buf.at[j], ag_buf.at[j], ag_ssem.at[0], ag_rsem.at[j], here).wait_recv()

        return c

    lax.fori_loop(0, owners, ag_wait, 0)
    for j in range(owners):
        sums[pl.ds(j * piece, piece), :] = ag_buf[j].astype(F32) * scale
    one, two, rest = (sums[pl.ds(i * tall, tall), :] for i in range(3))
    one_parts = (one, pltpu.roll(one, chans, 1), rest)
    two_parts = (two, pltpu.roll(two, chans, 1), pltpu.roll(rest, chans, 1))
    for a in range(3):
        cut = slice(a * chans, (a + 1) * chans)
        for b in range(3):
            g1_ref[b, a] = one_parts[b][cut, :chans]
            g2_ref[2 - a, 2 - b] = two_parts[b][cut, :chans]

    @pl.when(owns)
    def _():
        def sent(k, c):
            ag_copy(k).wait_send()
            return c

        lax.fori_loop(1, group, sent, 0)

    out_copy.wait()
    df_copy.wait()


def on_device(
    nlon, nlat, fields_in, weight_one, weight_two, cotangent,
    north_map, north_code, south_map, south_code,
):
    chans, rows, cols = fields_in.shape
    scale = 1.0 / math.sqrt(float(rows * cols * nlon * nlat))
    tall = 3 * chans
    planes = 2 if nlat % 2 == 0 else 1
    group, depth = nlon * planes, nlat // planes
    owners = max(k for k in range(1, group + 1) if 3 * tall % (8 * k) == 0)
    piece = 3 * tall // owners
    vmem = pl.BlockSpec(memory_space=pltpu.VMEM)
    smem = pl.BlockSpec(memory_space=pltpu.SMEM)
    hbm = pl.BlockSpec(memory_space=pltpu.HBM)
    wide = pltpu.VMEM(((rows + 2) * chans, 2 * LANES), BF16)
    flat16 = pltpu.VMEM((chans * rows, LANES), BF16)
    flat32 = pltpu.VMEM((chans * rows, LANES), F32)
    polar = pltpu.VMEM((nlon, chans, LANES), BF16)
    dma = pltpu.SemaphoreType.DMA
    scratch = [
        flat16, flat16,
        pltpu.VMEM((9 * chans, chans), BF16), pltpu.VMEM((9 * chans, chans), BF16),
        flat16, flat16, flat32, flat32, wide, wide, wide, wide, flat32,
        pltpu.VMEM((4, tall, tall), BF16), pltpu.VMEM((6, tall, tall), BF16),
        pltpu.VMEM((chans, 2 * LANES), BF16),
        pltpu.VMEM((4, 3, chans, LANES), BF16), pltpu.VMEM((4, 8, chans, LANES), BF16),
        polar, polar, polar, polar,
        pltpu.VMEM((tall, 2 * LANES), F32), pltpu.VMEM((tall, 2 * LANES), F32),
        pltpu.VMEM((3 * tall, LANES), F32),
        pltpu.VMEM((owners, piece, LANES), BF16), pltpu.VMEM((group, piece, LANES), BF16),
        pltpu.VMEM((piece, LANES), BF16), pltpu.VMEM((depth, piece, LANES), BF16),
        pltpu.VMEM((owners, piece, LANES), BF16),
        dma((6,)), dma((4, 8)), dma((4, 8)), dma((4, nlon)), dma((4, nlon)),
        dma((owners,)), dma((group,)), dma((depth,)), dma((depth,)),
        dma((group,)), dma((owners,)),
    ]
    output, d_fields, grad_one, grad_two = pl.pallas_call(
        functools.partial(kernel, nlon, nlat, planes, rows, chans, owners, scale),
        out_shape=(
            jax.ShapeDtypeStruct((chans * rows, cols), BF16),
            jax.ShapeDtypeStruct((chans * rows, cols), BF16),
            jax.ShapeDtypeStruct((3, 3, chans, chans), F32),
            jax.ShapeDtypeStruct((3, 3, chans, chans), F32),
        ),
        in_specs=[hbm, hbm, hbm, hbm, smem, smem, smem, smem],
        out_specs=(hbm, hbm, vmem, vmem),
        scratch_shapes=scratch,
        compiler_params=pltpu.CompilerParams(
            collective_id=0, has_side_effects=True, vmem_limit_bytes=48 * 1024 * 1024
        ),
    )(
        fields_in.reshape(chans * rows, cols), cotangent.reshape(chans * rows, cols),
        weight_one.reshape(9 * chans, chans), weight_two.reshape(9 * chans, chans),
        north_map, north_code, south_map, south_code,
    )
    shape = (chans, rows, cols)
    return (output.reshape(shape), d_fields.reshape(shape), grad_one, grad_two)


def solution(mesh):
    placed = (P(None, "lat", "lon"), P(), P(), P(None, "lat", "lon"), P(), P(), P(), P())
    return jax.shard_map(
        functools.partial(on_device, mesh.shape["lon"], mesh.shape["lat"]),
        mesh=mesh,
        in_specs=placed,
        out_specs=(P(None, "lat", "lon"), P(None, "lat", "lon"), P(), P()),
        check_vma=False,
    )
```

time: 58.5 us -> 56.4 us (0.964)
  Pallas kernels: 50 us -> 47.9 us
    pallas_call x1, Pallas kernels: 50 us -> 47.9 us  [on_device(): pl.pallas_call(functools.partial(kernel, nlon, nlat, planes, rows, chans,...]
where the time goes in v3:
time: 56.4 us; the launch traced here: 56.1 us
  Pallas kernels  47.9 us (85%)
  local copies, waits for them, and re-layouts  7.59 us (13%)
  between operations  0.68 us (1%)
    pallas_call x1, Pallas kernels, on_device(): pl.pallas_call(functools.partial(kernel, nlon, nlat, planes, rows, chans,...  47.9 us
    unnamed x20, local copies, waits for them, and re-layouts  7.59 us

profile of v3, /device:TPU:1, one launch (start us, length us, event | category | flops | bytes accessed | tf_op | source)
XLA Modules:
  0.0 56.1 jit_solution(12267548856452078362)
XLA Ops:
  0.6 0.0 copy-start.7
  0.6 0.0 copy-start.4
  0.7 0.0 copy-start.5
  0.7 0.0 copy-start.6
  0.7 0.6 %copy-done.7 = s32[16]{0:T(128)S(1)} copy-done((s32[16]{0:T(128)S(1)}, s32[16]{0:T(128)}, u32[]{:S(2)}) %copy-start.7) | copy-done | bytes 88
  1.3 0.0 copy-done.4
  1.3 0.0 copy-done.5
  1.3 0.0 copy-done.6
  1.3 0.0 copy-start
  1.3 1.0 %copy-done = bf16[64,32,128]{2,1,0:T(8,128)(2,1)S(1)} copy-done((bf16[64,32,128]{2,1,0:T(8,128)(2,1)S(1)}, bf16[64,32,128]{2,1,0:T(8,128)(2,1)}, u32[]{:S(2)}) %copy-start) | copy-done | bytes 524312
  2.4 0.0 copy-start.1
  2.4 1.0 %copy-done.1 = bf16[64,32,128]{2,1,0:T(8,128)(2,1)S(1)} copy-done((bf16[64,32,128]{2,1,0:T(8,128)(2,1)S(1)}, bf16[64,32,128]{2,1,0:T(8,128)(2,1)}, u32[]{:S(2)}) %copy-start.1) | copy-done | bytes 524312
  3.4 0.0 copy-start.2
  3.4 0.9 %copy-done.2 = bf16[3,3,64,64]{3,2,1,0:T(8,128)(2,1)S(1)} copy-done((bf16[3,3,64,64]{3,2,1,0:T(8,128)(2,1)S(1)}, bf16[3,3,64,64]{3,2,1,0:T(8,128)(2,1)}, u32[]{:S(2)}) %copy-start.2) | copy-done | bytes 73752
  4.3 0.0 copy-start.3
  4.3 0.9 %copy-done.3 = bf16[3,3,64,64]{3,2,1,0:T(8,128)(2,1)S(1)} copy-done((bf16[3,3,64,64]{3,2,1,0:T(8,128)(2,1)S(1)}, bf16[3,3,64,64]{3,2,1,0:T(8,128)(2,1)}, u32[]{:S(2)}) %copy-start.3) | copy-done | bytes 73752
  5.2 47.9 %shard_map.111 = (bf16[2048,128]{1,0:T(8,128)(2,1)S(1)}, bf16[2048,128]{1,0:T(8,128)(2,1)S(1)}, f32[3,3,64,64]{3,2,1,0:T(8,128)S(1)}, f32[3,3,64,64]{3,2,1,0:T(8,128)S(1)}) custom-call(bf16[2048,128]{1,0:T(8,128)(2,1)S(1)} %bitcast.6, bf16[2048,128]{1,0:T(8,128)(2,1)S(1)} %bitcast.7, bf16[576,64]{1,0:T(8,128)(2,1)S(1)} %bitcast.10, ...), custom_call_target="tpu_custom_call" | custom-call | tf_op jit(solution)/shard_map/pallas_call | solution.py:688
  53.1 0.8 %copy.16 = bf16[64,32,128]{2,1,0:T(8,128)(2,1)} copy(bf16[64,32,128]{2,1,0:T(8,128)(2,1)S(1)} %bitcast.9) | data formatting | bytes 1048576
  53.9 0.8 %copy.17 = bf16[64,32,128]{2,1,0:T(8,128)(2,1)} copy(bf16[64,32,128]{2,1,0:T(8,128)(2,1)S(1)} %bitcast.8) | data formatting | bytes 1048576
  54.7 0.7 %copy.18 = f32[3,3,64,64]{3,2,1,0:T(8,128)} copy(f32[3,3,64,64]{3,2,1,0:T(8,128)S(1)} %get-tuple-element.18) | data formatting | bytes 294912
  55.4 0.7 %copy.19 = f32[3,3,64,64]{3,2,1,0:T(8,128)} copy(f32[3,3,64,64]{3,2,1,0:T(8,128)S(1)} %get-tuple-element.19) | data formatting | bytes 294912
Async XLA Ops:
  0.6 0.7 %copy-start.7 = (s32[16]{0:T(128)S(1)}, s32[16]{0:T(128)}, u32[]{:S(2)}) copy-start(s32[16]{0:T(128)} %south_code.1) | copy-start | bytes 196
  0.6 0.7 %copy-start.4 = (s32[16]{0:T(128)S(1)}, s32[16]{0:T(128)}, u32[]{:S(2)}) copy-start(s32[16]{0:T(128)} %north_map.1) | copy-start | bytes 196
  0.7 0.7 %copy-start.5 = (s32[16]{0:T(128)S(1)}, s32[16]{0:T(128)}, u32[]{:S(2)}) copy-start(s32[16]{0:T(128)} %north_code.1) | copy-start | bytes 196
  0.7 0.7 %copy-start.6 = (s32[16]{0:T(128)S(1)}, s32[16]{0:T(128)}, u32[]{:S(2)}) copy-start(s32[16]{0:T(128)} %south_map.1) | copy-start | bytes 196
  1.3 1.0 %copy-start = (bf16[64,32,128]{2,1,0:T(8,128)(2,1)S(1)}, bf16[64,32,128]{2,1,0:T(8,128)(2,1)}, u32[]{:S(2)}) copy-start(bf16[64,32,128]{2,1,0:T(8,128)(2,1)} %param.8) | copy-start | bytes 1572868
  2.4 1.0 %copy-start.1 = (bf16[64,32,128]{2,1,0:T(8,128)(2,1)S(1)}, bf16[64,32,128]{2,1,0:T(8,128)(2,1)}, u32[]{:S(2)}) copy-start(bf16[64,32,128]{2,1,0:T(8,128)(2,1)} %param.11) | copy-start | bytes 1572868
  3.4 0.9 %copy-start.2 = (bf16[3,3,64,64]{3,2,1,0:T(8,128)(2,1)S(1)}, bf16[3,3,64,64]{3,2,1,0:T(8,128)(2,1)}, u32[]{:S(2)}) copy-start(bf16[3,3,64,64]{3,2,1,0:T(8,128)(2,1)} %param.9) | copy-start | bytes 221188
  4.3 0.9 %copy-start.3 = (bf16[3,3,64,64]{3,2,1,0:T(8,128)(2,1)S(1)}, bf16[3,3,64,64]{3,2,1,0:T(8,128)(2,1)}, u32[]{:S(2)}) copy-start(bf16[3,3,64,64]{3,2,1,0:T(8,128)(2,1)} %param.10) | copy-start | bytes 221188

commit v4 on v3

--- a/solution.py
+++ b/solution.py
@@ -14,6 +14,7 @@
 BF16 = jnp.bfloat16
 NT = (((1,), (1,)), ((), ()))
 FIELDS, COT, HIDDEN, DPRE = range(4)
+VMEM_BYTES = 48 * 1024 * 1024
 
 
 def aligned(start, step):
@@ -23,8 +24,8 @@
 def kernel(
     nlon, nlat, planes, rows, chans, owners, scale,
     fields_hbm, cot_hbm, one_hbm, two_hbm, north_map, north_code, south_map, south_code,
-    out_hbm, df_hbm, g1_ref, g2_ref,
-    fields_in, cot_in, one_ref, two_ref, out_buf, df_buf,
+    out_ref, df_ref, g1_ref, g2_ref,
+    fields_in, cot_in, one_ref, two_ref,
     stage, stage_two, fwide, gwide, hwide, dwide, slope, w_ref, wedge, rim_row,
     send, recv, pole_f, pole_c, pole_h, pole_d, acc_one, acc_two, sums,
     rs_send, rs_recv, ar_send, ar_recv, ag_buf,
@@ -532,9 +533,7 @@
         return c
 
     lax.fori_loop(0, rows, out_row, 0, unroll=rows)
-    out_buf[...] = stage[...].astype(BF16)
-    out_copy = pltpu.make_async_copy(out_buf, out_hbm, local_sem.at[4])
-    out_copy.start()
+    out_ref[...] = stage[...].astype(BF16)
 
     def ar_copy(k):
         return put(ar_send, ar_recv.at[z], ar_ssem.at[k], ar_rsem.at[z], along_z(k))
@@ -569,9 +568,7 @@
         return c
 
     lax.fori_loop(0, rows, df_row, 0, unroll=rows)
-    df_buf[...] = stage_two[...].astype(BF16)
-    df_copy = pltpu.make_async_copy(df_buf, df_hbm, local_sem.at[5])
-    df_copy.start()
+    df_ref[...] = stage_two[...].astype(BF16)
 
     def ag_copy(k):
         return put(
@@ -645,8 +642,17 @@
 
         lax.fori_loop(1, group, sent, 0)
 
-    out_copy.wait()
-    df_copy.wait()
+
+def hand_over(*refs):
+    count = (len(refs) - 1) // 2
+    sems = refs[-1]
+    copies = [
+        pltpu.make_async_copy(refs[i], refs[count + i], sems.at[i]) for i in range(count)
+    ]
+    for copy in copies:
+        copy.start()
+    for copy in copies:
+        copy.wait()
 
 
 def on_device(
@@ -668,10 +674,14 @@
     flat32 = pltpu.VMEM((chans * rows, LANES), F32)
     polar = pltpu.VMEM((nlon, chans, LANES), BF16)
     dma = pltpu.SemaphoreType.DMA
+
+    def in_hbm(x):
+        return pltpu.with_memory_space_constraint(x, pltpu.HBM)
+
     scratch = [
         flat16, flat16,
         pltpu.VMEM((9 * chans, chans), BF16), pltpu.VMEM((9 * chans, chans), BF16),
-        flat16, flat16, flat32, flat32, wide, wide, wide, wide, flat32,
+        flat32, flat32, wide, wide, wide, wide, flat32,
         pltpu.VMEM((4, tall, tall), BF16), pltpu.VMEM((6, tall, tall), BF16),
         pltpu.VMEM((chans, 2 * LANES), BF16),
         pltpu.VMEM((4, 3, chans, LANES), BF16), pltpu.VMEM((4, 8, chans, LANES), BF16),
@@ -681,29 +691,36 @@
         pltpu.VMEM((owners, piece, LANES), BF16), pltpu.VMEM((group, piece, LANES), BF16),
         pltpu.VMEM((piece, LANES), BF16), pltpu.VMEM((depth, piece, LANES), BF16),
         pltpu.VMEM((owners, piece, LANES), BF16),
-        dma((6,)), dma((4, 8)), dma((4, 8)), dma((4, nlon)), dma((4, nlon)),
+        dma((4,)), dma((4, 8)), dma((4, 8)), dma((4, nlon)), dma((4, nlon)),
         dma((owners,)), dma((group,)), dma((depth,)), dma((depth,)),
         dma((group,)), dma((owners,)),
     ]
-    output, d_fields, grad_one, grad_two = pl.pallas_call(
+    results = pl.pallas_call(
         functools.partial(kernel, nlon, nlat, planes, rows, chans, owners, scale),
         out_shape=(
-            jax.ShapeDtypeStruct((chans * rows, cols), BF16),
-            jax.ShapeDtypeStruct((chans * rows, cols), BF16),
-            jax.ShapeDtypeStruct((3, 3, chans, chans), F32),
-            jax.ShapeDtypeStruct((3, 3, chans, chans), F32),
+            pltpu.VMEM((chans * rows, cols), BF16),
+            pltpu.VMEM((chans * rows, cols), BF16),
+            pltpu.VMEM((3, 3, chans, chans), F32),
+            pltpu.VMEM((3, 3, chans, chans), F32),
         ),
         in_specs=[hbm, hbm, hbm, hbm, smem, smem, smem, smem],
-        out_specs=(hbm, hbm, vmem, vmem),
+        out_specs=(vmem, vmem, vmem, vmem),
         scratch_shapes=scratch,
         compiler_params=pltpu.CompilerParams(
-            collective_id=0, has_side_effects=True, vmem_limit_bytes=48 * 1024 * 1024
+            collective_id=0, has_side_effects=True, vmem_limit_bytes=VMEM_BYTES
         ),
     )(
-        fields_in.reshape(chans * rows, cols), cotangent.reshape(chans * rows, cols),
-        weight_one.reshape(9 * chans, chans), weight_two.reshape(9 * chans, chans),
+        in_hbm(fields_in.reshape(chans * rows, cols)), in_hbm(cotangent.reshape(chans * rows, cols)),
+        in_hbm(weight_one.reshape(9 * chans, chans)), in_hbm(weight_two.reshape(9 * chans, chans)),
         north_map, north_code, south_map, south_code,
     )
+    output, d_fields, grad_one, grad_two = pl.pallas_call(
+        hand_over,
+        out_shape=tuple(jax.ShapeDtypeStruct(x.shape, x.dtype) for x in results),
+        in_specs=[vmem] * 4,
+        out_specs=(hbm,) * 4,
+        scratch_shapes=[dma((4,))],
+    )(*[pltpu.with_memory_space_constraint(x, pltpu.VMEM) for x in results])
     shape = (chans, rows, cols)
     return (output.reshape(shape), d_fields.reshape(shape), grad_one, grad_two)
 

time: 56.4 us -> 50.5 us (0.90)
  local copies, waits for them, and re-layouts: 7.59 us -> 0.67 us
  Pallas kernels: 47.9 us -> 49 us
    unnamed x20 -> x8, local copies, waits for them, and re-layouts: 7.59 us -> 0.67 us
    pallas_call x0 -> x1, Pallas kernels: none -> 1.19 us  [on_device(): pl.pallas_call(hand_over, out_shape=tuple((jax.ShapeDtypeStruct(x.shape,...]
where the time goes in v4:
time: 50.5 us; the launch traced here: 50.4 us
  Pallas kernels  49 us (97%)
  between operations  0.68 us (1%)
  local copies, waits for them, and re-layouts  0.67 us (1%)
    pallas_call x1, Pallas kernels, on_device(): pl.pallas_call(functools.partial(kernel, nlon, nlat, planes, rows, chans,...  47.8 us
    pallas_call x1, Pallas kernels, on_device(): pl.pallas_call(hand_over, out_shape=tuple((jax.ShapeDtypeStruct(x.shape,...  1.19 us

profile of v4, /device:TPU:1, one launch (start us, length us, event | category | flops | bytes accessed | tf_op | source)
XLA Modules:
  0.0 50.4 jit_solution(4875770518433552049)
XLA Ops:
  0.6 0.0 copy-start.3
  0.6 0.0 copy-start
  0.7 0.0 copy-start.1
  0.7 0.0 copy-start.2
  0.7 0.6 %copy-done.3 = s32[16]{0:T(128)S(1)} copy-done((s32[16]{0:T(128)S(1)}, s32[16]{0:T(128)}, u32[]{:S(2)}) %copy-start.3) | copy-done | bytes 88
  1.3 0.0 copy-done
  1.3 0.0 copy-done.1
  1.3 0.0 copy-done.2
  1.3 47.8 %shard_map.111 = (bf16[2048,128]{1,0:T(8,128)(2,1)S(1)}, bf16[2048,128]{1,0:T(8,128)(2,1)S(1)}, f32[3,3,64,64]{3,2,1,0:T(8,128)S(1)}, f32[3,3,64,64]{3,2,1,0:T(8,128)S(1)}) custom-call(bf16[2048,128]{1,0:T(8,128)(2,1)} %bitcast.6, bf16[2048,128]{1,0:T(8,128)(2,1)} %bitcast.7, bf16[576,64]{1,0:T(8,128)(2,1)} %bitcast.8, bf16[576,64]{1,0:T(8,128)(2,1)} %bitcast.9, ...), custom_call_target="tpu_custom_call" | custom-call | tf_op jit(solution)/shard_map/pallas_call | solution.py:698
  49.2 1.2 %shard_map.112 = (bf16[2048,128]{1,0:T(8,128)(2,1)}, bf16[2048,128]{1,0:T(8,128)(2,1)}, f32[3,3,64,64]{3,2,1,0:T(8,128)}, f32[3,3,64,64]{3,2,1,0:T(8,128)}) custom-call(bf16[2048,128]{1,0:T(8,128)(2,1)S(1)} %get-tuple-element.12.refs_0_, bf16[2048,128]{1,0:T(8,128)(2,1)S(1)} %get-tuple-element.13.refs_1_, f32[3,3,64,64]{3,2,1,0:T(8,128)S(1)} %get-tuple-element.14.refs_2_, ...), custom_call_target="tpu_custom_call" | custom-call | tf_op jit(solution)/shard_map/pallas_call | solution.py:717
Async XLA Ops:
  0.6 0.7 %copy-start.3 = (s32[16]{0:T(128)S(1)}, s32[16]{0:T(128)}, u32[]{:S(2)}) copy-start(s32[16]{0:T(128)} %south_code.1) | copy-start | bytes 196
  0.6 0.7 %copy-start = (s32[16]{0:T(128)S(1)}, s32[16]{0:T(128)}, u32[]{:S(2)}) copy-start(s32[16]{0:T(128)} %north_map.1) | copy-start | bytes 196
  0.7 0.7 %copy-start.1 = (s32[16]{0:T(128)S(1)}, s32[16]{0:T(128)}, u32[]{:S(2)}) copy-start(s32[16]{0:T(128)} %north_code.1) | copy-start | bytes 196
  0.7 0.7 %copy-start.2 = (s32[16]{0:T(128)S(1)}, s32[16]{0:T(128)}, u32[]{:S(2)}) copy-start(s32[16]{0:T(128)} %south_map.1) | copy-start | bytes 196

commit v5 on v4

--- a/solution.py
+++ b/solution.py
@@ -29,7 +29,7 @@
     stage, stage_two, fwide, gwide, hwide, dwide, slope, w_ref, wedge, rim_row,
     send, recv, pole_f, pole_c, pole_h, pole_d, acc_one, acc_two, sums,
     rs_send, rs_recv, ar_send, ar_recv, ag_buf,
-    local_sem, near_send, near_recv, pole_send, pole_recv,
+    local_sem, near_send, near_recv, pole_send, pole_recv, hand_send, hand_recv,
     rs_ssem, rs_rsem, ar_ssem, ar_rsem, ag_ssem, ag_rsem,
 ):
     lon = lax.axis_index("lon")
@@ -136,11 +136,37 @@
         ]
         return sides, up, down
 
+    half = nlon // 2
+    core = lax.rem(lon, 2)
+    chip = lax.div(lon, 2)
+    sibling = (lat, lon + 1 - 2 * core)
+
+    def strip_at(k):
+        return lax.rem(k, 2) * half + lax.div(k, 2)
+
     def pole_copy(x, part, k):
         return put(
-            send.at[x, part], pole[x].at[lon], pole_send.at[x, k], pole_recv.at[x, lon],
-            (lat, lax.rem(lon + k, nlon)),
-        )
+            send.at[x, part], pole[x].at[core * half + chip], pole_send.at[x, k],
+            pole_recv.at[x, chip], (lat, lax.rem(lon + 2 * k, nlon)),
+        )
+
+    def hand_on(x, at):
+        block = pole[x].at[pl.ds(at * half, half)]
+        return put(block, block, hand_send.at[x], hand_recv.at[x], sibling)
+
+    def forward_poles(x):
+        @pl.when(at_pole)
+        def _():
+            def step(k, c):
+                source = lax.rem(chip + k, half)
+                put(
+                    send.at[x, 0], pole[x].at[core * half + source], pole_send.at[x, k],
+                    pole_recv.at[x, source], here,
+                ).wait_recv()
+                return c
+
+            lax.fori_loop(1, half, step, 0)
+            hand_on(x, core).start()
 
     def start_exchange(x):
         sides, up, down = near_copies(x)
@@ -162,8 +188,8 @@
                 pole_copy(x, part, k).start()
                 return c
 
-            lax.fori_loop(1, nlon, step, 0)
-            pole[x][lon] = send[x, part]
+            lax.fori_loop(1, half, step, 0)
+            pole[x][core * half + chip] = send[x, part]
 
         @pl.when(at_top)
         def _():
@@ -191,15 +217,7 @@
 
         @pl.when(at_pole)
         def _():
-            def step(k, c):
-                source = lax.rem(lon + k, nlon)
-                put(
-                    send.at[x, 0], pole[x].at[source], pole_send.at[x, k],
-                    pole_recv.at[x, source], here,
-                ).wait_recv()
-                return c
-
-            lax.fori_loop(1, nlon, step, 0)
+            hand_on(x, 1 - core).wait_recv()
 
     def wait_sent(x):
         sides, up, down = near_copies(x)
@@ -222,7 +240,8 @@
                 pole_copy(x, 0, k).wait_send()
                 return c
 
-            lax.fori_loop(1, nlon, step, 0)
+            lax.fori_loop(1, half, step, 0)
+            hand_on(x, core).wait_send()
 
     def map_at(k):
         return jnp.where(at_top, north_map[k], south_map[k])
@@ -268,11 +287,10 @@
         keep = jnp.logical_or(lane == 2 * h, lane == lax.rem(2 * h + LANES - 1, LANES))
         return jnp.where(keep, pltpu.roll(value, 2 * h, 1), packed)
 
-    def send_edges(x, wide, packed):
+    def set_edges(x, wide, packed):
         send[x, 0] = wide[pl.ds(chans, chans), own]
         send[x, 1] = wide[pl.ds(rows * chans, chans), own]
         send[x, 2] = packed.astype(BF16)
-        start_exchange(x)
 
     none = jnp.zeros((chans, LANES), F32)
 
@@ -299,11 +317,11 @@
 
         def across(row):
             if forward:
-                strips = [turned(pole[x][map_at(k)], code_at(k)) for k in (west, lon, east)]
+                strips = [turned(pole[x][strip_at(map_at(k))], code_at(k)) for k in (west, lon, east)]
                 set_ghost_row(wide, row, *strips)
                 return
             before, mid, after = [
-                turned(pole[x][lax.rem(rim_source + shift, nlon)], rim_code)
+                turned(pole[x][strip_at(lax.rem(rim_source + shift, nlon))], rim_code)
                 for shift in (nlon - 1, 0, 1)
             ]
             flip = rim_code == 1
@@ -397,36 +415,47 @@
         )
         return [first.astype(BF16), second.astype(BF16)]
 
-    def gradient(shift_wide, window_wide, acc, shifted_first):
-        count = min(16, rows)
+    def gradient(shift_wide, window_wide, acc, shifted_first, hs):
+        moved, windows = [], []
+        for h in hs:
+            moved += shifted(shift_wide, h)
+            windows.append(window_wide[pl.ds(aligned(h, chans), tall), :])
+        moved, windows = jnp.concatenate(moved, axis=1), jnp.concatenate(windows, axis=1)
+        a, b = (moved, windows) if shifted_first else (windows, moved)
+        acc[:, :tall] += lax.dot_general(a, b, NT, preferred_element_type=F32)
+
+    def inner_gradient(shift_wide, window_wide, acc, shifted_first):
+        count = (rows - 2) // 2
 
         def step(i, c):
-            moved, windows = [], []
-            for u in range(count):
-                h = i * count + u
-                moved += shifted(shift_wide, h)
-                windows.append(window_wide[pl.ds(aligned(h, chans), tall), :])
-            moved, windows = jnp.concatenate(moved, axis=1), jnp.concatenate(windows, axis=1)
-            a, b = (moved, windows) if shifted_first else (windows, moved)
-            acc[:, :tall] += lax.dot_general(a, b, NT, preferred_element_type=F32)
+            first = 1 + i * count
+            gradient(
+                shift_wide, window_wide, acc, shifted_first, [first + u for u in range(count)]
+            )
             return c
 
         acc[...] = jnp.zeros_like(acc)
-        lax.fori_loop(0, rows // count, step, 0)
-
-    def all_rows(row, x, wide, forward):
-        set_ghost_cols(x, wide)
-        carry = lax.fori_loop(1, rows - 1, row, none, unroll=rows - 2)
-        set_ghost_rows(x, wide, forward)
-        return lax.fori_loop(0, 2, lambda k, c: row(k * (rows - 1), c), carry, unroll=2)
+        lax.fori_loop(0, 2, step, 0)
+
+    ends = (0, rows - 1)
+
+    def inner_rows(row, carry):
+        return lax.fori_loop(1, rows - 1, row, carry, unroll=rows - 2)
+
+    def end_rows(row, carry):
+        for h in ends:
+            carry = row(h, carry)
+        return carry
 
     loads[0].wait()
     packed = take_in(fields_in, stage, fwide)
+    set_edges(FIELDS, fwide, packed)
     pl.semaphore_wait(barrier, group - 1 + depth - 1 + beside)
-    send_edges(FIELDS, fwide, packed)
+    start_exchange(FIELDS)
     loads[1].wait()
     packed = take_in(cot_in, stage_two, gwide)
-    send_edges(COT, gwide, packed)
+    set_edges(COT, gwide, packed)
+    start_exchange(COT)
     loads[2].wait()
     loads[3].wait()
     weight_forms()
@@ -446,9 +475,6 @@
         hwide[pl.ds(aligned(h + 1, chans), chans), own] = value.astype(BF16)
         return pack_edge(h, value, packed)
 
-    packed = all_rows(hidden_row, FIELDS, fwide, True)
-    send_edges(HIDDEN, hwide, packed)
-
     def weights_at(kernel_at, h):
         place = jnp.where(h == 0, 0, jnp.where(h == rows - 1, 2, 1))
         return wedge[kernel_at * 3 + place]
@@ -459,11 +485,6 @@
         dwide[pl.ds(aligned(h + 1, chans), chans), own] = value.astype(BF16)
         return pack_edge(h, value, packed)
 
-    packed = all_rows(back_row, COT, gwide, False)
-    send_edges(DPRE, dwide, packed)
-
-    gradient(dwide, fwide, acc_one, True)
-
     def set_aside(row):
         place = pl.ds(row * chans, chans)
         rim_row[...] = gwide[place, :]
@@ -480,6 +501,20 @@
             rim_row[...], chosen, NT, preferred_element_type=F32
         )
 
+    set_ghost_cols(FIELDS, fwide)
+    hidden_packed = inner_rows(hidden_row, none)
+    forward_poles(FIELDS)
+    set_ghost_cols(COT, gwide)
+    d_packed = inner_rows(back_row, none)
+    forward_poles(COT)
+    inner_gradient(dwide, fwide, acc_one, True)
+    inner_gradient(hwide, gwide, acc_two, False)
+    set_ghost_rows(FIELDS, fwide, True)
+    hidden_packed = end_rows(hidden_row, hidden_packed)
+    set_ghost_rows(COT, gwide, False)
+    d_packed = end_rows(back_row, d_packed)
+    gradient(dwide, fwide, acc_one, True, ends)
+
     @pl.when(at_top)
     def _():
         set_aside(0)
@@ -488,7 +523,7 @@
     def _():
         set_aside(rows + 1)
 
-    gradient(hwide, gwide, acc_two, False)
+    gradient(hwide, gwide, acc_two, False, ends)
 
     @pl.when(at_top)
     def _():
@@ -525,15 +560,21 @@
     def _():
         rs_recv[mine] = rs_send[own_piece]
 
-    set_ghost_cols(HIDDEN, hwide)
-    set_ghost_rows(HIDDEN, hwide, True)
+    set_edges(HIDDEN, hwide, hidden_packed)
+    start_exchange(HIDDEN)
+    set_edges(DPRE, dwide, d_packed)
+    start_exchange(DPRE)
 
     def out_row(h, c):
         stage[pl.ds(h, chans, stride=rows), :] = conv_row(w_ref[1], hwide, h)
         return c
 
-    lax.fori_loop(0, rows, out_row, 0, unroll=rows)
-    out_ref[...] = stage[...].astype(BF16)
+    def df_row(h, c):
+        stage_two[pl.ds(h, chans, stride=rows), :] = conv_row(weights_at(0, h), dwide, h)
+        return c
+
+    set_ghost_cols(HIDDEN, hwide)
+    inner_rows(out_row, 0)
 
     def ar_copy(k):
         return put(ar_send, ar_recv.at[z], ar_ssem.at[k], ar_rsem.at[z], along_z(k))
@@ -560,14 +601,15 @@
 
         lax.fori_loop(1, depth, start, 0)
 
+    forward_poles(HIDDEN)
+    forward_poles(DPRE)
     set_ghost_cols(DPRE, dwide)
+    inner_rows(df_row, 0)
+    set_ghost_rows(HIDDEN, hwide, True)
+    end_rows(out_row, 0)
     set_ghost_rows(DPRE, dwide, False)
-
-    def df_row(h, c):
-        stage_two[pl.ds(h, chans, stride=rows), :] = conv_row(weights_at(0, h), dwide, h)
-        return c
-
-    lax.fori_loop(0, rows, df_row, 0, unroll=rows)
+    end_rows(df_row, 0)
+    out_ref[...] = stage[...].astype(BF16)
     df_ref[...] = stage_two[...].astype(BF16)
 
     def ag_copy(k):
@@ -691,7 +733,7 @@
         pltpu.VMEM((owners, piece, LANES), BF16), pltpu.VMEM((group, piece, LANES), BF16),
         pltpu.VMEM((piece, LANES), BF16), pltpu.VMEM((depth, piece, LANES), BF16),
         pltpu.VMEM((owners, piece, LANES), BF16),
-        dma((4,)), dma((4, 8)), dma((4, 8)), dma((4, nlon)), dma((4, nlon)),
+        dma((4,)), dma((4, 8)), dma((4, 8)), dma((4, nlon // 2)), dma((4, nlon // 2)), dma((4,)), dma((4,)),
         dma((owners,)), dma((group,)), dma((depth,)), dma((depth,)),
         dma((group,)), dma((owners,)),
     ]

time: 50.5 us -> 45.8 us (0.907)
  Pallas kernels: 49 us -> 44.4 us
    pallas_call x1, Pallas kernels: 47.8 us -> 43.2 us  [on_device(): pl.pallas_call(functools.partial(kernel, nlon, nlat, planes, rows, chans,...]
where the time goes in v5:
time: 45.8 us; the launch traced here: 45.7 us
  Pallas kernels  44.4 us (97%)
  between operations  0.68 us (1%)
  local copies, waits for them, and re-layouts  0.67 us (1%)
    pallas_call x1, Pallas kernels, on_device(): pl.pallas_call(functools.partial(kernel, nlon, nlat, planes, rows, chans,...  43.2 us
    pallas_call x1, Pallas kernels, on_device(): pl.pallas_call(hand_over, out_shape=tuple((jax.ShapeDtypeStruct(x.shape,...  1.19 us

profile of v5, /device:TPU:1, one launch (start us, length us, event | category | flops | bytes accessed | tf_op | source)
XLA Modules:
  0.0 45.7 jit_solution(7318602122064299440)
XLA Ops:
  0.6 0.0 copy-start.3
  0.6 0.0 copy-start
  0.7 0.0 copy-start.1
  0.7 0.0 copy-start.2
  0.7 0.6 %copy-done.3 = s32[16]{0:T(128)S(1)} copy-done((s32[16]{0:T(128)S(1)}, s32[16]{0:T(128)}, u32[]{:S(2)}) %copy-start.3) | copy-done | bytes 88
  1.3 0.0 copy-done
  1.3 0.0 copy-done.1
  1.3 0.0 copy-done.2
  1.3 43.2 %shard_map.111 = (bf16[2048,128]{1,0:T(8,128)(2,1)S(1)}, bf16[2048,128]{1,0:T(8,128)(2,1)S(1)}, f32[3,3,64,64]{3,2,1,0:T(8,128)S(1)}, f32[3,3,64,64]{3,2,1,0:T(8,128)S(1)}) custom-call(bf16[2048,128]{1,0:T(8,128)(2,1)} %bitcast.6, bf16[2048,128]{1,0:T(8,128)(2,1)} %bitcast.7, bf16[576,64]{1,0:T(8,128)(2,1)} %bitcast.8, bf16[576,64]{1,0:T(8,128)(2,1)} %bitcast.9, ...), custom_call_target="tpu_custom_call" | custom-call | tf_op jit(solution)/shard_map/pallas_call | solution.py:740
  44.5 1.2 %shard_map.112 = (bf16[2048,128]{1,0:T(8,128)(2,1)}, bf16[2048,128]{1,0:T(8,128)(2,1)}, f32[3,3,64,64]{3,2,1,0:T(8,128)}, f32[3,3,64,64]{3,2,1,0:T(8,128)}) custom-call(bf16[2048,128]{1,0:T(8,128)(2,1)S(1)} %get-tuple-element.12.refs_0_, bf16[2048,128]{1,0:T(8,128)(2,1)S(1)} %get-tuple-element.13.refs_1_, f32[3,3,64,64]{3,2,1,0:T(8,128)S(1)} %get-tuple-element.14.refs_2_, ...), custom_call_target="tpu_custom_call" | custom-call | tf_op jit(solution)/shard_map/pallas_call | solution.py:759
Async XLA Ops:
  0.6 0.7 %copy-start.3 = (s32[16]{0:T(128)S(1)}, s32[16]{0:T(128)}, u32[]{:S(2)}) copy-start(s32[16]{0:T(128)} %south_code.1) | copy-start | bytes 196
  0.6 0.7 %copy-start = (s32[16]{0:T(128)S(1)}, s32[16]{0:T(128)}, u32[]{:S(2)}) copy-start(s32[16]{0:T(128)} %north_map.1) | copy-start | bytes 196
  0.7 0.7 %copy-start.1 = (s32[16]{0:T(128)S(1)}, s32[16]{0:T(128)}, u32[]{:S(2)}) copy-start(s32[16]{0:T(128)} %north_code.1) | copy-start | bytes 196
  0.7 0.7 %copy-start.2 = (s32[16]{0:T(128)S(1)}, s32[16]{0:T(128)}, u32[]{:S(2)}) copy-start(s32[16]{0:T(128)} %south_map.1) | copy-start | bytes 196

commit v6 on v5

--- a/solution.py
+++ b/solution.py
@@ -23,9 +23,9 @@
 
 def kernel(
     nlon, nlat, planes, rows, chans, owners, scale,
-    fields_hbm, cot_hbm, one_hbm, two_hbm, north_map, north_code, south_map, south_code,
+    fields_hbm, cot_hbm, one_hbm, two_hbm, nmap_hbm, ncode_hbm, smap_hbm, scode_hbm,
     out_ref, df_ref, g1_ref, g2_ref,
-    fields_in, cot_in, one_ref, two_ref,
+    fields_in, cot_in, one_ref, two_ref, north_map, north_code, south_map, south_code,
     stage, stage_two, fwide, gwide, hwide, dwide, slope, w_ref, wedge, rim_row,
     send, recv, pole_f, pole_c, pole_h, pole_d, acc_one, acc_two, sums,
     rs_send, rs_recv, ar_send, ar_recv, ag_buf,
@@ -66,12 +66,27 @@
     def owner_at(j):
         return lax.div(j, 3) * 4 + lax.rem(j, 3) if spread_owners else j
 
-    if spread_owners:
-        owns = lax.rem(mine, 4) < 3
-        own_piece = lax.div(mine, 4) * 3 + lax.rem(mine, 4)
+    def ownership(g):
+        if spread_owners:
+            return lax.rem(g, 4) < 3, lax.div(g, 4) * 3 + lax.rem(g, 4)
+        return g < owners, g
+
+    owns, own_piece = ownership(mine)
+
+    if group == 32 and planes == 2:
+        far = {0: 0, 1: 1, 2: 2, 3: 1}
+        steps = [(x, y, c, h) for x in range(4) for y in range(2) for c in range(2) for h in range(2)]
+        steps = sorted(steps[1:], key=lambda t: -(far[t[0]] + (2 * t[3] - t[1] if t[3] else t[1])))
+        others = [
+            lax.rem(lax.div(lon, 4) + x, 4) * 4
+            + lax.rem(lax.rem(lax.div(lon, 2), 2) + y, 2) * 2
+            + lax.rem(lax.rem(lon, 2) + c, 2)
+            + nlon * lax.rem(plane + h, 2)
+            for x, y, c, h in steps
+        ]
     else:
-        owns = mine < owners
-        own_piece = mine
+        others = [lax.rem(mine + k, group) for k in range(1, group)]
+    z_steps = sorted(range(1, depth), key=lambda k: -min(k, depth - k))
 
     barrier = pltpu.get_barrier_semaphore()
 
@@ -105,7 +120,11 @@
     loads = [
         pltpu.make_async_copy(source, target, local_sem.at[i])
         for i, (source, target) in enumerate(
-            [(fields_hbm, fields_in), (cot_hbm, cot_in), (one_hbm, one_ref), (two_hbm, two_ref)]
+            [
+                (fields_hbm, fields_in), (cot_hbm, cot_in), (one_hbm, one_ref), (two_hbm, two_ref),
+                (nmap_hbm, north_map), (ncode_hbm, north_code),
+                (smap_hbm, south_map), (scode_hbm, south_code),
+            ]
         )
     ]
     for load in loads:
@@ -183,6 +202,7 @@
             for copy in down:
                 copy.start()
 
+    def start_poles(x):
         def pole_start(part):
             def step(k, c):
                 pole_copy(x, part, k).start()
@@ -252,8 +272,6 @@
     def find_owner(k, c):
         hit = map_at(k) == lon
         return jnp.where(hit, k, c[0]), jnp.where(hit, code_at(k), c[1])
-
-    rim_source, rim_code = lax.fori_loop(0, nlon, find_owner, (jnp.int32(0), jnp.int32(0)))
 
     def turned(row, code):
         i = lax.broadcasted_iota(jnp.int32, (LANES, LANES), 0)
@@ -452,12 +470,15 @@
     set_edges(FIELDS, fwide, packed)
     pl.semaphore_wait(barrier, group - 1 + depth - 1 + beside)
     start_exchange(FIELDS)
+    start_poles(FIELDS)
     loads[1].wait()
     packed = take_in(cot_in, stage_two, gwide)
     set_edges(COT, gwide, packed)
     start_exchange(COT)
-    loads[2].wait()
-    loads[3].wait()
+    start_poles(COT)
+    for load in loads[2:]:
+        load.wait()
+    rim_source, rim_code = lax.fori_loop(0, nlon, find_owner, (jnp.int32(0), jnp.int32(0)))
     weight_forms()
     rim_weights()
 
@@ -510,19 +531,19 @@
     inner_gradient(dwide, fwide, acc_one, True)
     inner_gradient(hwide, gwide, acc_two, False)
     set_ghost_rows(FIELDS, fwide, True)
+    set_ghost_rows(COT, gwide, False)
     hidden_packed = end_rows(hidden_row, hidden_packed)
-    set_ghost_rows(COT, gwide, False)
     d_packed = end_rows(back_row, d_packed)
+
+    @pl.when(at_top)
+    def _():
+        set_aside(0)
+
+    @pl.when(at_bottom)
+    def _():
+        set_aside(rows + 1)
+
     gradient(dwide, fwide, acc_one, True, ends)
-
-    @pl.when(at_top)
-    def _():
-        set_aside(0)
-
-    @pl.when(at_bottom)
-    def _():
-        set_aside(rows + 1)
-
     gradient(hwide, gwide, acc_two, False, ends)
 
     @pl.when(at_top)
@@ -547,14 +568,15 @@
             rs_send.at[j], rs_recv.at[mine], rs_ssem.at[j], rs_rsem.at[mine], in_group(owner_at(j))
         )
 
-    def rs_start(j, c):
-        @pl.when(owner_at(j) != mine)
-        def _():
-            rs_copy(j).start()
-
-        return c
-
-    lax.fori_loop(0, owners, rs_start, 0)
+    for other in others:
+        takes, taken = ownership(other)
+
+        @pl.when(takes)
+        def _():
+            put(
+                rs_send.at[taken], rs_recv.at[mine], rs_ssem.at[taken], rs_rsem.at[mine],
+                in_group(other),
+            ).start()
 
     @pl.when(owns)
     def _():
@@ -595,27 +617,18 @@
         ar_send[...] = total.astype(BF16)
         ar_recv[z] = total.astype(BF16)
 
-        def start(k, c):
+        for k in z_steps:
             ar_copy(k).start()
-            return c
-
-        lax.fori_loop(1, depth, start, 0)
-
-    forward_poles(HIDDEN)
-    forward_poles(DPRE)
+
+    start_poles(HIDDEN)
+    start_poles(DPRE)
     set_ghost_cols(DPRE, dwide)
     inner_rows(df_row, 0)
-    set_ghost_rows(HIDDEN, hwide, True)
-    end_rows(out_row, 0)
-    set_ghost_rows(DPRE, dwide, False)
-    end_rows(df_row, 0)
-    out_ref[...] = stage[...].astype(BF16)
-    df_ref[...] = stage_two[...].astype(BF16)
 
     def ag_copy(k):
         return put(
             ag_buf.at[own_piece], ag_buf.at[own_piece], ag_ssem.at[k], ag_rsem.at[own_piece],
-            in_group(group_peer(k)),
+            in_group(others[k]),
         )
 
     @pl.when(owns)
@@ -631,11 +644,17 @@
             total = total + ar_recv[k].astype(F32)
         ag_buf[own_piece] = total.astype(BF16)
 
-        def start(k, c):
+        for k in range(group - 1):
             ag_copy(k).start()
-            return c
-
-        lax.fori_loop(1, group, start, 0)
+
+    forward_poles(HIDDEN)
+    forward_poles(DPRE)
+    set_ghost_rows(HIDDEN, hwide, True)
+    set_ghost_rows(DPRE, dwide, False)
+    end_rows(out_row, 0)
+    end_rows(df_row, 0)
+    out_ref[...] = stage[...].astype(BF16)
+    df_ref[...] = stage_two[...].astype(BF16)
 
     for x in range(4):
         wait_sent(x)
@@ -678,11 +697,8 @@
 
     @pl.when(owns)
     def _():
-        def sent(k, c):
+        for k in range(group - 1):
             ag_copy(k).wait_send()
-            return c
-
-        lax.fori_loop(1, group, sent, 0)
 
 
 def hand_over(*refs):
@@ -709,12 +725,12 @@
     owners = max(k for k in range(1, group + 1) if 3 * tall % (8 * k) == 0)
     piece = 3 * tall // owners
     vmem = pl.BlockSpec(memory_space=pltpu.VMEM)
-    smem = pl.BlockSpec(memory_space=pltpu.SMEM)
     hbm = pl.BlockSpec(memory_space=pltpu.HBM)
     wide = pltpu.VMEM(((rows + 2) * chans, 2 * LANES), BF16)
     flat16 = pltpu.VMEM((chans * rows, LANES), BF16)
     flat32 = pltpu.VMEM((chans * rows, LANES), F32)
     polar = pltpu.VMEM((nlon, chans, LANES), BF16)
+    maps = pltpu.SMEM((nlon,), jnp.int32)
     dma = pltpu.SemaphoreType.DMA
 
     def in_hbm(x):
@@ -723,6 +739,7 @@
     scratch = [
         flat16, flat16,
         pltpu.VMEM((9 * chans, chans), BF16), pltpu.VMEM((9 * chans, chans), BF16),
+        maps, maps, maps, maps,
         flat32, flat32, wide, wide, wide, wide, flat32,
         pltpu.VMEM((4, tall, tall), BF16), pltpu.VMEM((6, tall, tall), BF16),
         pltpu.VMEM((chans, 2 * LANES), BF16),
@@ -733,7 +750,7 @@
         pltpu.VMEM((owners, piece, LANES), BF16), pltpu.VMEM((group, piece, LANES), BF16),
         pltpu.VMEM((piece, LANES), BF16), pltpu.VMEM((depth, piece, LANES), BF16),
         pltpu.VMEM((owners, piece, LANES), BF16),
-        dma((4,)), dma((4, 8)), dma((4, 8)), dma((4, nlon // 2)), dma((4, nlon // 2)), dma((4,)), dma((4,)),
+        dma((8,)), dma((4, 8)), dma((4, 8)), dma((4, nlon // 2)), dma((4, nlon // 2)), dma((4,)), dma((4,)),
         dma((owners,)), dma((group,)), dma((depth,)), dma((depth,)),
         dma((group,)), dma((owners,)),
     ]
@@ -745,7 +762,7 @@
             pltpu.VMEM((3, 3, chans, chans), F32),
             pltpu.VMEM((3, 3, chans, chans), F32),
         ),
-        in_specs=[hbm, hbm, hbm, hbm, smem, smem, smem, smem],
+        in_specs=[hbm] * 8,
         out_specs=(vmem, vmem, vmem, vmem),
         scratch_shapes=scratch,
         compiler_params=pltpu.CompilerParams(
@@ -754,7 +771,7 @@
     )(
         in_hbm(fields_in.reshape(chans * rows, cols)), in_hbm(cotangent.reshape(chans * rows, cols)),
         in_hbm(weight_one.reshape(9 * chans, chans)), in_hbm(weight_two.reshape(9 * chans, chans)),
-        north_map, north_code, south_map, south_code,
+        in_hbm(north_map), in_hbm(north_code), in_hbm(south_map), in_hbm(south_code),
     )
     output, d_fields, grad_one, grad_two = pl.pallas_call(
         hand_over,

time: 45.8 us -> 42.8 us (0.934)
  Pallas kernels: 44.4 us -> 42 us
  local copies, waits for them, and re-layouts: 0.67 us -> 0 us
    pallas_call x1, Pallas kernels: 43.2 us -> 40.8 us  [on_device(): pl.pallas_call(functools.partial(kernel, nlon, nlat, planes, rows, chans,...]
    unnamed x8 -> x0, local copies, waits for them, and re-layouts: 0.67 us -> none
where the time goes in v6:
time: 42.8 us; the launch traced here: 42.7 us
  Pallas kernels  42 us (98%)
  between operations  0.64 us (1%)
    pallas_call x1, Pallas kernels, on_device(): pl.pallas_call(functools.partial(kernel, nlon, nlat, planes, rows, chans,...  40.8 us
    pallas_call x1, Pallas kernels, on_device(): pl.pallas_call(hand_over, out_shape=tuple((jax.ShapeDtypeStruct(x.shape,...  1.19 us

profile of v6, /device:TPU:1, one launch (start us, length us, event | category | flops | bytes accessed | tf_op | source)
XLA Modules:
  0.0 42.7 jit_solution(6884625167289418235)
XLA Ops:
  0.6 40.8 %shard_map.111 = (bf16[2048,128]{1,0:T(8,128)(2,1)S(1)}, bf16[2048,128]{1,0:T(8,128)(2,1)S(1)}, f32[3,3,64,64]{3,2,1,0:T(8,128)S(1)}, f32[3,3,64,64]{3,2,1,0:T(8,128)S(1)}) custom-call(bf16[2048,128]{1,0:T(8,128)(2,1)} %bitcast.6, bf16[2048,128]{1,0:T(8,128)(2,1)} %bitcast.7, bf16[576,64]{1,0:T(8,128)(2,1)} %bitcast.8, bf16[576,64]{1,0:T(8,128)(2,1)} %bitcast.9, ...), custom_call_target="tpu_custom_call" | custom-call | tf_op jit(solution)/shard_map/pallas_call | solution.py:757
  41.5 1.2 %shard_map.112 = (bf16[2048,128]{1,0:T(8,128)(2,1)}, bf16[2048,128]{1,0:T(8,128)(2,1)}, f32[3,3,64,64]{3,2,1,0:T(8,128)}, f32[3,3,64,64]{3,2,1,0:T(8,128)}) custom-call(bf16[2048,128]{1,0:T(8,128)(2,1)S(1)} %get-tuple-element.12.refs_0_, bf16[2048,128]{1,0:T(8,128)(2,1)S(1)} %get-tuple-element.13.refs_1_, f32[3,3,64,64]{3,2,1,0:T(8,128)S(1)} %get-tuple-element.14.refs_2_, ...), custom_call_target="tpu_custom_call" | custom-call | tf_op jit(solution)/shard_map/pallas_call | solution.py:776

commit v7 on v6

--- a/solution.py
+++ b/solution.py
@@ -30,7 +30,7 @@
     send, recv, pole_f, pole_c, pole_h, pole_d, acc_one, acc_two, sums,
     rs_send, rs_recv, ar_send, ar_recv, ag_buf,
     local_sem, near_send, near_recv, pole_send, pole_recv, hand_send, hand_recv,
-    rs_ssem, rs_rsem, ar_ssem, ar_rsem, ag_ssem, ag_rsem,
+    rs_ssem, rs_rsem, ar_ssem, ar_rsem, ag_ssem, ag_rsem, told,
 ):
     lon = lax.axis_index("lon")
     lat = lax.axis_index("lat")
@@ -113,8 +113,45 @@
         for at in (west, lon, east):
             greet((lat + 1, at))
 
-    lax.fori_loop(1, group, greet_group, 0)
-    lax.fori_loop(1, depth, greet_z, 0)
+    relayed = planes == 2 and 4 <= depth <= 8
+    partner = ((1 - plane) * depth + z, lon)
+    if relayed:
+        def greet_row(k, c):
+            greet((lat, lax.rem(lon + k, nlon)))
+            return c
+
+        lax.fori_loop(1, nlon, greet_row, 0)
+        for place in (along_z(1), along_z(depth - 1), partner):
+            greet(place)
+        greeted = nlon - 1 + 3
+    else:
+        lax.fori_loop(1, group, greet_group, 0)
+        lax.fori_loop(1, depth, greet_z, 0)
+        greeted = group - 1 + depth - 1
+
+    def tell(at, place):
+        pl.semaphore_signal(
+            told.at[at], inc=1, device_id={"lat": place[0], "lon": place[1]}, device_id_type=MESH
+        )
+
+    def tell_near():
+        if relayed:
+            tell(0, along_z(1))
+            tell(1, along_z(depth - 1))
+            tell(2, partner)
+
+    def tell_far():
+        if relayed:
+            for at in range(3):
+                pl.semaphore_wait(told.at[at], 1)
+            tell(3, along_z(2))
+            tell(4, along_z(depth - 2))
+
+    def all_told():
+        if relayed:
+            for at in (3, 4):
+                pl.semaphore_wait(told.at[at], 1)
+
     beside = 3 * has_north.astype(jnp.int32) + 3 * has_south.astype(jnp.int32)
 
     loads = [
@@ -468,9 +505,10 @@
     loads[0].wait()
     packed = take_in(fields_in, stage, fwide)
     set_edges(FIELDS, fwide, packed)
-    pl.semaphore_wait(barrier, group - 1 + depth - 1 + beside)
+    pl.semaphore_wait(barrier, greeted + beside)
     start_exchange(FIELDS)
     start_poles(FIELDS)
+    tell_near()
     loads[1].wait()
     packed = take_in(cot_in, stage_two, gwide)
     set_edges(COT, gwide, packed)
@@ -524,10 +562,12 @@
 
     set_ghost_cols(FIELDS, fwide)
     hidden_packed = inner_rows(hidden_row, none)
+    tell_far()
     forward_poles(FIELDS)
     set_ghost_cols(COT, gwide)
     d_packed = inner_rows(back_row, none)
     forward_poles(COT)
+    all_told()
     inner_gradient(dwide, fwide, acc_one, True)
     inner_gradient(hwide, gwide, acc_two, False)
     set_ghost_rows(FIELDS, fwide, True)
@@ -752,7 +792,7 @@
         pltpu.VMEM((owners, piece, LANES), BF16),
         dma((8,)), dma((4, 8)), dma((4, 8)), dma((4, nlon // 2)), dma((4, nlon // 2)), dma((4,)), dma((4,)),
         dma((owners,)), dma((group,)), dma((depth,)), dma((depth,)),
-        dma((group,)), dma((owners,)),
+        dma((group,)), dma((owners,)), pltpu.SemaphoreType.REGULAR((5,)),
     ]
     results = pl.pallas_call(
         functools.partial(kernel, nlon, nlat, planes, rows, chans, owners, scale),

time: 42.8 us -> 41.9 us (0.979)
  Pallas kernels: 42 us -> 41.2 us
    pallas_call x1, Pallas kernels: 40.8 us -> 40 us  [on_device(): pl.pallas_call(functools.partial(kernel, nlon, nlat, planes, rows, chans,...]
where the time goes in v7:
time: 41.9 us; the launch traced here: 41.8 us
  Pallas kernels  41.2 us (98%)
  between operations  0.64 us (2%)
    pallas_call x1, Pallas kernels, on_device(): pl.pallas_call(functools.partial(kernel, nlon, nlat, planes, rows, chans,...  40 us
    pallas_call x1, Pallas kernels, on_device(): pl.pallas_call(hand_over, out_shape=tuple((jax.ShapeDtypeStruct(x.shape,...  1.19 us

profile of v7, /device:TPU:1, one launch (start us, length us, event | category | flops | bytes accessed | tf_op | source)
XLA Modules:
  0.0 41.8 jit_solution(919361396812077999)
XLA Ops:
  0.6 40.0 %shard_map.111 = (bf16[2048,128]{1,0:T(8,128)(2,1)S(1)}, bf16[2048,128]{1,0:T(8,128)(2,1)S(1)}, f32[3,3,64,64]{3,2,1,0:T(8,128)S(1)}, f32[3,3,64,64]{3,2,1,0:T(8,128)S(1)}) custom-call(bf16[2048,128]{1,0:T(8,128)(2,1)} %bitcast.6, bf16[2048,128]{1,0:T(8,128)(2,1)} %bitcast.7, bf16[576,64]{1,0:T(8,128)(2,1)} %bitcast.8, bf16[576,64]{1,0:T(8,128)(2,1)} %bitcast.9, ...), custom_call_target="tpu_custom_call" | custom-call | tf_op jit(solution)/shard_map/pallas_call | solution.py:797
  40.6 1.2 %shard_map.112 = (bf16[2048,128]{1,0:T(8,128)(2,1)}, bf16[2048,128]{1,0:T(8,128)(2,1)}, f32[3,3,64,64]{3,2,1,0:T(8,128)}, f32[3,3,64,64]{3,2,1,0:T(8,128)}) custom-call(bf16[2048,128]{1,0:T(8,128)(2,1)S(1)} %get-tuple-element.12.refs_0_, bf16[2048,128]{1,0:T(8,128)(2,1)S(1)} %get-tuple-element.13.refs_1_, f32[3,3,64,64]{3,2,1,0:T(8,128)S(1)} %get-tuple-element.14.refs_2_, ...), custom_call_target="tpu_custom_call" | custom-call | tf_op jit(solution)/shard_map/pallas_call | solution.py:816

commit v8 on v7

--- a/solution.py
+++ b/solution.py
@@ -575,6 +575,31 @@
     hidden_packed = end_rows(hidden_row, hidden_packed)
     d_packed = end_rows(back_row, d_packed)
 
+    gradient(dwide, fwide, acc_one, True, ends)
+    early = tall // piece
+
+    def rs_copy(j):
+        return put(
+            rs_send.at[j], rs_recv.at[mine], rs_ssem.at[j], rs_rsem.at[mine], in_group(owner_at(j))
+        )
+
+    def send_pieces(first, end):
+        for j in range(first, end):
+            rs_send[j] = sums[pl.ds(j * piece, piece), :].astype(BF16)
+        for other in others:
+            takes, taken = ownership(other)
+            due = jnp.logical_and(taken >= first, taken < end)
+
+            @pl.when(jnp.logical_and(takes, due))
+            def _():
+                put(
+                    rs_send.at[taken], rs_recv.at[mine], rs_ssem.at[taken], rs_rsem.at[mine],
+                    in_group(other),
+                ).start()
+
+    sums[pl.ds(0, tall), :] = acc_one[:, :LANES]
+    send_pieces(0, early)
+
     @pl.when(at_top)
     def _():
         set_aside(0)
@@ -583,7 +608,6 @@
     def _():
         set_aside(rows + 1)
 
-    gradient(dwide, fwide, acc_one, True, ends)
     gradient(hwide, gwide, acc_two, False, ends)
 
     @pl.when(at_top)
@@ -594,29 +618,12 @@
     def _():
         credit(rows - 1, 0)
 
-    sums[pl.ds(0, tall), :] = acc_one[:, :LANES]
     sums[pl.ds(tall, tall), :] = acc_two[:, :LANES]
     half_lane = lax.broadcasted_iota(jnp.int32, (tall, LANES), 1) < chans
     sums[pl.ds(2 * tall, tall), :] = jnp.where(
         half_lane, acc_one[:, LANES:], pltpu.roll(acc_two[:, LANES:], chans, 1)
     )
-    for j in range(owners):
-        rs_send[j] = sums[pl.ds(j * piece, piece), :].astype(BF16)
-
-    def rs_copy(j):
-        return put(
-            rs_send.at[j], rs_recv.at[mine], rs_ssem.at[j], rs_rsem.at[mine], in_group(owner_at(j))
-        )
-
-    for other in others:
-        takes, taken = ownership(other)
-
-        @pl.when(takes)
-        def _():
-            put(
-                rs_send.at[taken], rs_recv.at[mine], rs_ssem.at[taken], rs_rsem.at[mine],
-                in_group(other),
-            ).start()
+    send_pieces(early, owners)
 
     @pl.when(owns)
     def _():

time: 41.9 us -> 42.9 us (1.024)
  Pallas kernels: 41.2 us -> 42.2 us
    pallas_call x1, Pallas kernels: 40 us -> 41 us  [on_device(): pl.pallas_call(functools.partial(kernel, nlon, nlat, planes, rows, chans,...]
where the time goes in v8:
time: 42.9 us; the launch traced here: 42.8 us
  Pallas kernels  42.2 us (98%)
  between operations  0.64 us (1%)
    pallas_call x1, Pallas kernels, on_device(): pl.pallas_call(functools.partial(kernel, nlon, nlat, planes, rows, chans,...  41 us
    pallas_call x1, Pallas kernels, on_device(): pl.pallas_call(hand_over, out_shape=tuple((jax.ShapeDtypeStruct(x.shape,...  1.19 us

profile of v8, /device:TPU:1, one launch (start us, length us, event | category | flops | bytes accessed | tf_op | source)
XLA Modules:
  0.0 42.8 jit_solution(2350278288554579)
XLA Ops:
  0.6 41.0 %shard_map.111 = (bf16[2048,128]{1,0:T(8,128)(2,1)S(1)}, bf16[2048,128]{1,0:T(8,128)(2,1)S(1)}, f32[3,3,64,64]{3,2,1,0:T(8,128)S(1)}, f32[3,3,64,64]{3,2,1,0:T(8,128)S(1)}) custom-call(bf16[2048,128]{1,0:T(8,128)(2,1)} %bitcast.6, bf16[2048,128]{1,0:T(8,128)(2,1)} %bitcast.7, bf16[576,64]{1,0:T(8,128)(2,1)} %bitcast.8, bf16[576,64]{1,0:T(8,128)(2,1)} %bitcast.9, ...), custom_call_target="tpu_custom_call" | custom-call | tf_op jit(solution)/shard_map/pallas_call | solution.py:804
  41.6 1.2 %shard_map.112 = (bf16[2048,128]{1,0:T(8,128)(2,1)}, bf16[2048,128]{1,0:T(8,128)(2,1)}, f32[3,3,64,64]{3,2,1,0:T(8,128)}, f32[3,3,64,64]{3,2,1,0:T(8,128)}) custom-call(bf16[2048,128]{1,0:T(8,128)(2,1)S(1)} %get-tuple-element.12.refs_0_, bf16[2048,128]{1,0:T(8,128)(2,1)S(1)} %get-tuple-element.13.refs_1_, f32[3,3,64,64]{3,2,1,0:T(8,128)S(1)} %get-tuple-element.14.refs_2_, ...), custom_call_target="tpu_custom_call" | custom-call | tf_op jit(solution)/shard_map/pallas_call | solution.py:823
